TPU v7x, 32 devices: a whole 2x2x4 slice. The times are simulated.
32 devices in a mesh: edge: 8 (over z, x), chan: 4 (over y, core).
Axes of the slice: x: 2, y: 2, z: 4, core: 2. Of those that a mesh axis runs over, the one named last changes fastest.
Arguments:
- edge_emb: bfloat16 [32768, 512], P('edge', 'chan'), may hold values from -6 to 6
- atom_emb: bfloat16 [1024, 256], P('edge'), may hold values from -6 to 6
- radial: bfloat16 [32768, 128], P('edge'), may hold values from 0 to 1
- circular: bfloat16 [16, 16, 32768], P(None, None, 'edge'), may hold values from -6 to 6
- spherical: bfloat16 [32, 8, 32768], P(None, None, 'edge'), may hold values from -6 to 6
- atom_tags: int32 [1024], P('edge'), may hold values from 0 to 2
- edge_source: int32 [32768], P('edge'), may hold values from 0 to 1023, as said below
- edge_target: int32 [32768], P('edge'), may hold values from 0 to 1023, as said below
- trip_source: int32 [16, 32768], P(None, 'edge'), may hold values from 0 to 12287, as said below
- trip_mask: int32 [16, 32768], P(None, 'edge'), may hold values from 0 to 1
- quad_source: int32 [8, 32768], P(None, 'edge'), may hold values from 0 to 12287, as said below
- quad_mask: int32 [8, 32768], P(None, 'edge'), may hold values from 0 to 1
- triplet_down_weight: bfloat16 [512, 64], P(None, 'chan'), may hold values from -0.25 to 0.25
- trip_radial: bfloat16 [128, 64], P(None, 'chan'), may hold values from -0.5 to 0.5
- triplet_bilinear_weight: bfloat16 [16, 64, 64], P(None, 'chan'), may hold values from -0.1875 to 0.1875
- trip_up: bfloat16 [64, 512], P(None, 'chan'), may hold values from -0.75 to 0.75
- quad_down: bfloat16 [512, 32], P(None, 'chan'), may hold values from -0.25 to 0.25
- quad_radial: bfloat16 [128, 32], P(None, 'chan'), may hold values from -0.5 to 0.5
- quad_bilinear: bfloat16 [32, 32, 32], P(None, 'chan'), may hold values from -0.1875 to 0.1875
- quad_up: bfloat16 [32, 512], P(None, 'chan'), may hold values from -1 to 1
- source_proj: bfloat16 [256, 512], P(None, 'chan'), may hold values from -0.375 to 0.375
- target_proj: bfloat16 [256, 512], P(None, 'chan'), may hold values from -0.375 to 0.375
- resid_first: bfloat16 [512, 512], P(None, 'chan'), may hold values from -0.25 to 0.25
- resid_second: bfloat16 [512, 512], P('chan'), may hold values from -0.25 to 0.25
- edge_to_atom: bfloat16 [512, 256], P('chan'), may hold values from -0.046875 to 0.046875
- atom_update: bfloat16 [256, 256], replicated, may hold values from -0.375 to 0.375
- output_first: bfloat16 [256, 256], replicated, may hold values from -0.375 to 0.375
- output_second: bfloat16 [256], replicated, may hold values from -0.375 to 0.375
- tag_table: bfloat16 [3, 256], replicated, may hold values from -3 to 3
- grad_edges: bfloat16 [32768, 512], P('edge', 'chan'), may hold values from -6 to 6
- grad_atoms: bfloat16 [1024, 256], P('edge'), may hold values from -6 to 6
- grad_energy: float32 [1024], P('edge'), may hold values from -6 to 6
Outputs:
- edges_out: bfloat16 [32768, 512], P('edge', 'chan')
- atoms_out: bfloat16 [1024, 256], P('edge')
- energy: float32 [1024], P('edge')
- edge_grad: float32 [32768, 512], P('edge', 'chan')
- atom_grad: float32 [1024, 256], P('edge')
- trip_down_grad: float32 [512, 64], P(None, 'chan')
- trip_radial_grad: float32 [128, 64], P(None, 'chan')
- trip_bilinear_grad: float32 [16, 64, 64], P(None, 'chan')
- trip_up_grad: float32 [64, 512], P(None, 'chan')
- quad_down_grad: float32 [512, 32], P(None, 'chan')
- quad_radial_grad: float32 [128, 32], P(None, 'chan')
- quad_bilinear_grad: float32 [32, 32, 32], P(None, 'chan')
- quad_up_grad: float32 [32, 512], P(None, 'chan')
- source_proj_grad: float32 [256, 512], P(None, 'chan')
- target_proj_grad: float32 [256, 512], P(None, 'chan')
- resid_first_grad: float32 [512, 512], P(None, 'chan')
- resid_second_grad: float32 [512, 512], P('chan')
- edge_to_atom_grad: float32 [512, 256], P('chan')
- atom_update_grad: float32 [256, 256], replicated
- output_first_grad: float32 [256, 256], replicated
- output_second_grad: float32 [256], replicated
- tag_table_grad: float32 [3, 256], replicated
Inputs may be any that keep to these rules, and one draw needn't show every extreme that they name: `edge_source`: partition q holds edges q * 4096 to (q + 1) * 4096 - 1 and atoms q * 128 to (q + 1) * 128 - 1. The source atom of an edge lies in the edge's partition or in the partition just before or after it, the partitions closing into a loop. `edge_target`: the target atom of an edge lies in the edge's own partition. `trip_source`: values below 4096 name an edge of the partition before the slot's edge, the next 4096 one of its own partition, the last 4096 one of the partition after it, the partitions closing into a loop. `quad_source`: values below 4096 name an edge of the partition before the slot's edge, the next 4096 one of its own partition, the last 4096 one of the partition after it, the partitions closing into a loop.
All inputs are finite; a program needn't handle non-finite values.
Results may differ from a plain program's by a relative error of at most 0.014.
Values may be sent and summed in bfloat16 or wider, within the bound.
No kernel may reach another device: no remote copies, remote signals or barrier semaphores. Data moves between devices by JAX's collectives and lax.ppermute only.
A program may use at most 320 MiB of HBM per device.

v0:
```python
import functools

import jax
import jax.numpy as jnp
from jax import lax
from jax.experimental import pallas as pl
from jax.experimental.pallas import tpu as pltpu
from jax.sharding import PartitionSpec as P

TAGS = 3
LANES = 128
BLOCK = 16
BF16 = jnp.bfloat16
F32 = jnp.float32
HIGHEST = lax.Precision.HIGHEST


def chan_swap(value, mask):
    count = lax.axis_size("chan")
    return lax.ppermute(value, "chan", [(i, i ^ mask) for i in range(count)])


def edge_swap(value, mask):
    count = lax.axis_size("edge")
    return lax.ppermute(value, "edge", [(i, i ^ mask) for i in range(count)])


def edge_shift(value, step):
    count = lax.axis_size("edge")
    return lax.ppermute(value, "edge", [(i, (i + step) % count) for i in range(count)])


def after(value, *others):
    return lax.optimization_barrier((value,) + others)[0]


def gather_direct(value):
    return [value] + [chan_swap(value, step) for step in (1, 2, 3)]


def pick(blocks, place):
    return lax.dynamic_index_in_dim(blocks, place, 0, keepdims=False)


def reorder(blocks, rank):
    low_bit = (rank & 1) == 1
    high_bit = (rank & 2) == 2
    first = [jnp.where(low_bit, blocks[i ^ 1], blocks[i]) for i in range(4)]
    return [jnp.where(high_bit, first[i ^ 2], first[i]) for i in range(4)]


def gather_chan(value):
    across = chan_swap(value, 2)
    beside = chan_swap(jnp.stack([value, across]), 1)
    return [value, beside[0], across, beside[1]]


def exchange(blocks, rank):
    got = [pick(blocks, rank)]
    for step in (1, 2, 3):
        got.append(chan_swap(pick(blocks, rank ^ step), step))
    return reorder(got, rank)


def silu_grad(pre_act):
    sigmoid = jax.nn.sigmoid(pre_act)
    return sigmoid * (1.0 + pre_act * (1.0 - sigmoid))


def matmul(first_op, second_op):
    return jnp.dot(first_op, second_op, preferred_element_type=F32)


def inner(first_op, second_op):
    return lax.dot_general(
        first_op, second_op, (((0,), (0,)), ((), ())), preferred_element_type=F32
    )


def outer(first_op, second_op):
    return lax.dot_general(
        first_op, second_op, (((1,), (1,)), ((), ())), preferred_element_type=F32
    )


def block_weights(basis_ref, block, diagonal):
    basis = basis_ref[block].astype(F32)
    count, width = basis.shape
    spread = jnp.broadcast_to(basis[:, None, :], (count, BLOCK, width))
    spread = spread.reshape(count * BLOCK, width)
    return jnp.where(diagonal, spread, 0.0).astype(BF16)


def diagonal_mask(rows, width):
    row = lax.broadcasted_iota(jnp.int32, (rows, width), 0) % BLOCK
    col = lax.broadcasted_iota(jnp.int32, (rows, width), 1) % BLOCK
    return row == col


def lane_groups(value, width):
    group = lax.broadcasted_iota(jnp.int32, value.shape, 1) // width
    zero = jnp.zeros_like(value)
    masked = [jnp.where(group == fold, value, zero) for fold in range(LANES // width)]
    return jnp.concatenate(masked, axis=0)


def gather_body(
    index_ref, packed_ref, basis_ref, bilinear_ref, agg_ref, sum_ref, table, rows_a, rows_b, *, folds
):
    pieces, piece_rows, _ = packed_ref.shape
    groups, edges, _ = sum_ref.shape
    basis_count = groups * folds
    width = LANES // folds
    slots = basis_ref.shape[2] // BLOCK
    step = min(piece_rows, 128)
    per_piece = piece_rows // step
    lane = lax.broadcasted_iota(jnp.int32, (step, LANES), 1) // width

    def unpack(turn, _):
        piece = turn // per_piece
        start = pl.multiple_of((turn % per_piece) * step, step)
        values = packed_ref[piece, pl.ds(start, step), :].astype(F32)
        turned = [values] + [
            pltpu.roll(values, shift * width, 1) for shift in range(1, folds)
        ]
        for fold in range(folds):
            place = pl.multiple_of((piece * folds + fold) * piece_rows + start, step)
            spread = turned[(0 - fold) % folds]
            for group in range(1, folds):
                spread = jnp.where(lane == group, turned[(group - fold) % folds], spread)
            table[pl.ds(place, step), :] = spread
        return 0

    lax.fori_loop(0, pieces * per_piece, unpack, 0)
    diagonal = diagonal_mask(basis_count * BLOCK, slots * BLOCK)

    def fetch(block, rows):
        base = block * BLOCK
        for slot in range(slots):
            for within in range(BLOCK):
                place = index_ref[slot * edges + base + within]
                at = slot * BLOCK + within
                rows[pl.ds(at, 1), :] = table[pl.ds(place, 1), :]

    def combine(block, rows):
        weights = block_weights(basis_ref, block, diagonal)
        each = groups * BLOCK
        joined = jnp.concatenate(
            [weights[fold * each : (fold + 1) * each] for fold in range(folds)], axis=1
        )
        got = matmul(joined, lane_groups(rows[...].astype(BF16), width)).astype(BF16)
        start = pl.multiple_of(block * BLOCK, BLOCK)
        sum_ref[:, pl.ds(start, BLOCK), :] = got.reshape(groups, BLOCK, LANES)

    blocks = edges // BLOCK
    fetch(0, rows_a)

    def turn(pair, _):
        fetch(2 * pair + 1, rows_b)
        combine(2 * pair, rows_a)
        fetch(jnp.minimum(2 * pair + 2, blocks - 1), rows_a)
        combine(2 * pair + 1, rows_b)
        return 0

    lax.fori_loop(0, blocks // 2, turn, 0)
    total = matmul(sum_ref[0], bilinear_ref[0])
    for group in range(1, groups):
        total = total + matmul(sum_ref[group], bilinear_ref[group])
    agg_ref[...] = total.astype(BF16)


def branch_forward(index, packed, basis, bilinear, name):
    groups, _, out_width = bilinear.shape
    edges = basis.shape[0] * BLOCK
    folds = basis.shape[1] // groups
    vmem = pl.BlockSpec(memory_space=pltpu.VMEM)
    return pl.pallas_call(
        functools.partial(gather_body, folds=folds),
        out_shape=(
            jax.ShapeDtypeStruct((edges, out_width), BF16),
            jax.ShapeDtypeStruct((groups, edges, LANES), BF16),
        ),
        in_specs=[pl.BlockSpec(memory_space=pltpu.SMEM), vmem, vmem, vmem],
        out_specs=(vmem, vmem),
        scratch_shapes=[
            pltpu.VMEM((packed.shape[0] * edges, LANES), F32),
            pltpu.VMEM((basis.shape[2], LANES), F32),
            pltpu.VMEM((basis.shape[2], LANES), F32),
        ],
        compiler_params=pltpu.CompilerParams(vmem_limit_bytes=56 << 20),
        cost_estimate=pl.CostEstimate(flops=20 * 10**9, transcendentals=0, bytes_accessed=10**7),
        name=name,
    )(index, packed, basis, bilinear)


TABLES = 4


def scatter_body(
    index_ref, basis_ref, grad_ref, bilinear_ref, packed_ref, part, rows_a, rows_b, *tables, folds
):
    pieces, piece_rows, _ = packed_ref.shape
    groups, edges, _ = part.shape
    basis_count = groups * folds
    width = LANES // folds
    slots = basis_ref.shape[2] // BLOCK
    chunk = 256
    table_rows = tables[0].shape[0]

    def clear(turn, _):
        start = pl.multiple_of(turn * chunk, chunk)
        for table in tables:
            table[pl.ds(start, chunk), :] = jnp.zeros((chunk, LANES), F32)
        return 0

    lax.fori_loop(0, table_rows // chunk, clear, 0)
    for group in range(groups):
        part[group] = outer(grad_ref[...], bilinear_ref[group]).astype(BF16)
    diagonal = diagonal_mask(basis_count * BLOCK, slots * BLOCK)

    def spread(block, rows):
        weights = block_weights(basis_ref, block, diagonal)
        start = pl.multiple_of(block * BLOCK, BLOCK)
        values = part[:, pl.ds(start, BLOCK), :].reshape(groups * BLOCK, LANES)
        rows[...] = inner(weights, lane_groups(values, width))

    def store(block, rows):
        base = block * BLOCK
        for slot in range(slots):
            for within in range(BLOCK):
                place = index_ref[slot * edges + base + within]
                at = slot * BLOCK + within
                table = tables[at % len(tables)]
                table[pl.ds(place, 1), :] += rows[pl.ds(at, 1), :]

    blocks = edges // BLOCK
    spread(0, rows_a)

    def turn(pair, _):
        spread(2 * pair + 1, rows_b)
        store(2 * pair, rows_a)
        spread(jnp.minimum(2 * pair + 2, blocks - 1), rows_a)
        store(2 * pair + 1, rows_b)
        return 0

    lax.fori_loop(0, blocks // 2, turn, 0)
    step = min(piece_rows, 128)
    per_piece = piece_rows // step
    lane = lax.broadcasted_iota(jnp.int32, (step, LANES), 1) // width

    def pack(turn, _):
        piece = turn // per_piece
        start = pl.multiple_of((turn % per_piece) * step, step)
        joined = jnp.zeros((step, LANES), F32)
        for fold in range(folds):
            place = pl.multiple_of((piece * folds + fold) * piece_rows + start, step)
            total = tables[0][pl.ds(place, step), :]
            for table in tables[1:]:
                total = total + table[pl.ds(place, step), :]
            shift = LANES // 2
            while shift >= width:
                total = total + pltpu.roll(total, shift, 1)
                shift //= 2
            joined = jnp.where(lane == fold, total, joined)
        packed_ref[piece, pl.ds(start, step), :] = joined.astype(BF16)
        return 0

    lax.fori_loop(0, pieces * per_piece, pack, 0)


def branch_backward(index, basis, grad, bilinear, pieces, name):
    edges = grad.shape[0]
    groups = bilinear.shape[0]
    folds = basis.shape[1] // groups
    vmem = pl.BlockSpec(memory_space=pltpu.VMEM)
    return pl.pallas_call(
        functools.partial(scatter_body, folds=folds),
        out_shape=jax.ShapeDtypeStruct((pieces, edges // folds, LANES), BF16),
        in_specs=[pl.BlockSpec(memory_space=pltpu.SMEM), vmem, vmem, vmem],
        out_specs=vmem,
        scratch_shapes=[
            pltpu.VMEM((groups, edges, LANES), BF16),
            pltpu.VMEM((basis.shape[2], LANES), F32),
            pltpu.VMEM((basis.shape[2], LANES), F32),
        ]
        + [pltpu.VMEM((pieces * edges, LANES), F32)] * TABLES,
        compiler_params=pltpu.CompilerParams(vmem_limit_bytes=58 << 20),
        cost_estimate=pl.CostEstimate(flops=20 * 10**9, transcendentals=0, bytes_accessed=10**7),
        name=name,
    )(index, basis, grad, bilinear)


def fold_lanes(rows):
    count, width = rows.shape
    folds = LANES // width
    each = count // folds
    return jnp.concatenate([rows[i * each : (i + 1) * each] for i in range(folds)], axis=1)


def unfold_lanes(packed, width):
    folds = LANES // width
    return jnp.concatenate([packed[:, i * width : (i + 1) * width] for i in range(folds)], axis=0)


def columns(array):
    return jnp.concatenate(
        [array[:, i : i + LANES] for i in range(0, array.shape[1], LANES)], axis=0
    )


def uncolumns(rows, width):
    each = rows.shape[0] * LANES // width
    return jnp.concatenate(
        [rows[i * each : (i + 1) * each] for i in range(width // LANES)], axis=1
    )


def slot_blocks(basis_vals, keep_mask):
    count, slots, edges = basis_vals.shape
    weighted = basis_vals * keep_mask.astype(BF16)[None]
    split = weighted.reshape(count, slots, edges // BLOCK, BLOCK)
    return jnp.transpose(split, (2, 0, 1, 3)).reshape(edges // BLOCK, count, slots * BLOCK)


def edge_reduce(rows):
    count = lax.axis_size("edge")
    rank = lax.axis_index("edge")
    steps = []
    size = 1
    while size < count:
        steps.append(size)
        size *= 2
    total = rows.shape[0]
    padded = -(-total // (16 * count)) * 16 * count
    value = jnp.pad(rows, ((0, padded - total), (0, 0)))
    for mask in steps:
        half = value.shape[0] // 2
        bit = (rank & mask) != 0
        keep = jnp.where(bit, value[half:], value[:half])
        send = jnp.where(bit, value[:half], value[half:])
        got = edge_swap(send, mask)
        value = (keep.astype(F32) + got.astype(F32)).astype(BF16)
    for mask in reversed(steps):
        bit = (rank & mask) != 0
        got = edge_swap(value, mask)
        value = jnp.concatenate(
            [jnp.where(bit, got, value), jnp.where(bit, value, got)], axis=0
        )
    return value[:total]


def edge_sum(value, kind):
    count = lax.axis_size("edge")
    size = 1
    while size < count:
        value = value + edge_swap(value.astype(kind), size).astype(F32)
        size *= 2
    return value


def per_device(
    edge_emb,
    atom_emb,
    radial,
    circular,
    spherical,
    atom_tags,
    edge_source,
    edge_target,
    trip_source,
    trip_mask,
    quad_source,
    quad_mask,
    triplet_down_weight,
    trip_radial,
    triplet_bilinear_weight,
    trip_up,
    quad_down,
    quad_radial,
    quad_bilinear,
    quad_up,
    source_proj,
    target_proj,
    resid_first,
    resid_second,
    edge_to_atom,
    atom_update,
    output_first,
    output_second,
    tag_table,
    grad_edges,
    grad_atoms,
    grad_energy,
):
    edges_here = edge_emb.shape[0]
    atoms_here = atom_emb.shape[0]
    parts = lax.axis_size("chan")
    edge_parts = lax.axis_size("edge")
    rank = lax.axis_index("chan")
    edge_rank = lax.axis_index("edge")
    edges = edges_here // parts
    cols = edge_emb.shape[1]
    start = rank * edges

    def own(array, axis):
        return lax.dynamic_slice_in_dim(array, start, edges, axis)

    own_edges = jnp.concatenate(exchange(edge_emb.reshape(parts, edges, cols), rank), axis=1)

    trip_cols = triplet_down_weight.shape[1]
    quad_cols = quad_down.shape[1]
    trip_out = triplet_bilinear_weight.shape[2]
    quad_out = quad_bilinear.shape[2]
    down_own = jnp.concatenate([triplet_down_weight, quad_down], axis=1)
    small = jnp.concatenate(
        [
            columns(
                jnp.concatenate(
                    [down_own, jnp.concatenate([trip_radial, quad_radial], axis=1)], axis=0
                ).T
            ),
            fold_lanes(triplet_bilinear_weight.reshape(-1, trip_out)),
            fold_lanes(quad_bilinear.reshape(-1, quad_out)),
        ],
        axis=0,
    )
    small = reorder(gather_direct(small), rank)
    channels = parts * cols
    long = channels + radial.shape[1]
    small_rows = (trip_cols + quad_cols) * long // LANES
    trip_bil_rows = triplet_bilinear_weight.size // LANES
    downs = jnp.stack([uncolumns(block[:small_rows], long) for block in small])
    trip_both = downs[:, :trip_cols].reshape(parts * trip_cols, -1).T
    quad_both = downs[:, trip_cols:].reshape(parts * quad_cols, -1).T
    both = jnp.concatenate([trip_both, quad_both], axis=1)
    down_full, radial_full = both[:channels], both[channels:]
    trip_width = trip_both.shape[1]
    quad_width = quad_both.shape[1]
    trip_folds = LANES // trip_width
    quad_folds = LANES // quad_width

    def group_rows(blocks, shape, folds):
        whole = jnp.concatenate(
            [unfold_lanes(block, shape[2]).reshape(shape) for block in blocks], axis=1
        )
        count, width, out = whole.shape
        split = whole.reshape(folds, count // folds, width, out)
        return jnp.transpose(split, (1, 0, 2, 3)).reshape(count // folds, folds * width, out)

    trip_bil = group_rows(
        [block[small_rows : small_rows + trip_bil_rows] for block in small],
        triplet_bilinear_weight.shape,
        trip_folds,
    )
    quad_bil = group_rows(
        [block[small_rows + trip_bil_rows :] for block in small],
        quad_bilinear.shape,
        quad_folds,
    )

    own_radial = own(radial, 0)
    down_pre = matmul(own_edges, down_full)
    radial_pre = matmul(own_radial, radial_full)
    dense = (jax.nn.silu(down_pre) * radial_pre).astype(BF16)
    trip_piece = fold_lanes(dense[:, :trip_width])
    quad_piece = fold_lanes(dense[:, trip_width:])
    trip_rows = trip_piece.shape[0]
    wire = jnp.concatenate([trip_piece, quad_piece], axis=0)
    before = edge_shift(wire, 1)
    after_wire = edge_shift(wire, -1)
    own_pieces = gather_chan(wire)
    sides = jnp.stack([before, after_wire])
    across = chan_swap(sides, 2)
    beside = chan_swap(jnp.stack([sides, across]), 1)
    side_pieces = [sides, beside[0], across, beside[1]]
    all_pieces = jnp.stack(
        [side[0] for side in side_pieces] + own_pieces + [side[1] for side in side_pieces]
    )
    trip_packed = all_pieces[:, :trip_rows]
    quad_packed = all_pieces[:, trip_rows:]

    large = jnp.concatenate(
        [
            trip_up,
            quad_up,
            source_proj,
            target_proj,
            resid_first,
            columns(resid_second),
            columns(edge_to_atom),
        ],
        axis=0,
    )
    large_rel = gather_chan(after(large, across))
    large = reorder(large_rel, rank)
    grad_blocks = after(grad_edges, large_rel[2]).reshape(parts, edges, cols)
    grad_two = jnp.concatenate(exchange(grad_blocks, rank), axis=1)
    sizes = [
        trip_up.shape[0],
        quad_up.shape[0],
        source_proj.shape[0],
        target_proj.shape[0],
        resid_first.shape[0],
        resid_second.size // LANES,
        edge_to_atom.size // LANES,
    ]

    def offsets_of(sizes):
        return [sum(sizes[:i]) for i in range(len(sizes) + 1)]

    offsets = offsets_of(sizes)

    def piece(item):
        return [block[offsets[item] : offsets[item + 1]] for block in large]

    trip_up_full = jnp.concatenate(piece(0), axis=1)
    quad_up_full = jnp.concatenate(piece(1), axis=1)
    proj_full = jnp.concatenate(
        [jnp.concatenate(piece(2), axis=1), jnp.concatenate(piece(3), axis=1)], axis=0
    )
    first_full = jnp.concatenate(piece(4), axis=1)
    second_full = jnp.concatenate(
        [uncolumns(block, resid_second.shape[1]) for block in piece(5)], axis=0
    )
    to_atom_full = jnp.concatenate(
        [uncolumns(block, edge_to_atom.shape[1]) for block in piece(6)], axis=0
    )

    tag_onehot = (atom_tags[:, None] == jnp.arange(TAGS)[None, :]).astype(F32)
    atom_full = atom_emb.astype(F32) + jnp.dot(
        tag_onehot, tag_table.astype(F32), precision=HIGHEST
    )
    atom_low = atom_full.astype(BF16)
    atom_wide = jnp.concatenate(
        [edge_shift(atom_low, 1), atom_low, edge_shift(atom_low, -1)], axis=0
    )
    atom_total = edge_parts * atoms_here
    source_local = (own(edge_source, 0) - (edge_rank - 1) * atoms_here) % atom_total
    target_local = own(edge_target, 0) - edge_rank * atoms_here
    source_hot = (source_local[:, None] == jnp.arange(3 * atoms_here)[None, :]).astype(BF16)
    target_hot = (target_local[:, None] == jnp.arange(atoms_here)[None, :]).astype(BF16)
    ends = jnp.concatenate(
        [
            matmul(source_hot, atom_wide).astype(BF16),
            matmul(target_hot, atom_low).astype(BF16),
        ],
        axis=1,
    )

    def places(source):
        local = own(source, 1)
        within = local % edges_here
        owner = (within // edges) ^ rank
        return ((local // edges_here) * edges_here + owner * edges + within % edges).reshape(-1)

    trip_index = places(trip_source)
    quad_index = places(quad_source)
    circular, spherical = lax.optimization_barrier((circular, spherical, wire))[:2]
    trip_basis = slot_blocks(own(circular, 2), own(trip_mask, 1))
    quad_basis = slot_blocks(own(spherical, 2), own(quad_mask, 1))
    trip_agg, trip_sum = branch_forward(
        trip_index, trip_packed, trip_basis, trip_bil, "trip_gather"
    )
    quad_agg, quad_sum = branch_forward(
        quad_index, quad_packed, quad_basis, quad_bil, "quad_gather"
    )

    message = matmul(ends, proj_full)
    trip_out_pre = matmul(trip_agg, trip_up_full)
    quad_out_pre = matmul(quad_agg, quad_up_full)
    hidden_one = (
        own_edges.astype(F32)
        + jax.nn.silu(trip_out_pre)
        + jax.nn.silu(quad_out_pre)
        + jax.nn.silu(message)
    )
    hidden_low = hidden_one.astype(BF16)
    first_pre = matmul(hidden_low, first_full)
    first_low = jax.nn.silu(first_pre).astype(BF16)
    second_pre = matmul(first_low, second_full)
    edges_low = (hidden_one + jax.nn.silu(second_pre)).astype(BF16)
    edge_sums = inner(target_hot, edges_low)
    sums_high = edge_sums.astype(BF16)
    sums_rest = (edge_sums - sums_high.astype(F32)).astype(BF16)
    atom_sum = matmul(sums_high, to_atom_full) + matmul(sums_rest, to_atom_full)
    atom_sum = atom_sum + chan_swap(atom_sum, 1)
    atom_sum = atom_sum + chan_swap(atom_sum, 2)

    atom_sum_low = atom_sum.astype(BF16)
    update_pre = matmul(atom_sum_low, atom_update)
    atoms_new = atom_full + jax.nn.silu(update_pre)
    atoms_low = atoms_new.astype(BF16)
    output_pre = matmul(atoms_low, output_first)
    output_low = jax.nn.silu(output_pre).astype(BF16)
    energy = matmul(output_low, output_second)
    output_second_grad = jnp.dot(grad_energy, output_low.astype(F32), precision=HIGHEST)
    output_grad = (
        grad_energy[:, None] * output_second.astype(F32)[None, :] * silu_grad(output_pre)
    ).astype(BF16)
    output_first_grad = inner(atoms_low, output_grad)
    atoms_new_grad = grad_atoms.astype(F32) + outer(output_grad, output_first)
    update_grad = (atoms_new_grad * silu_grad(update_pre)).astype(BF16)
    atom_update_grad = inner(atom_sum_low, update_grad)
    atom_sum_grad = outer(update_grad, atom_update).astype(BF16)

    edge_part_grad = matmul(target_hot, atom_sum_grad).astype(BF16)
    edge_to_atom_grad = inner(edges_low, edge_part_grad)
    two_grad = grad_two.astype(F32) + outer(edge_part_grad, to_atom_full)
    second_grad = (two_grad * silu_grad(second_pre)).astype(BF16)
    resid_second_grad = inner(first_low, second_grad)
    first_grad = (outer(second_grad, second_full) * silu_grad(first_pre)).astype(BF16)
    resid_first_grad = inner(hidden_low, first_grad)
    one_grad = two_grad + outer(first_grad, first_full)
    trip_out_grad = (one_grad * silu_grad(trip_out_pre)).astype(BF16)
    quad_out_grad = (one_grad * silu_grad(quad_out_pre)).astype(BF16)
    message_grad = (one_grad * silu_grad(message)).astype(BF16)
    trip_up_grad = inner(trip_agg, trip_out_grad)
    quad_up_grad = inner(quad_agg, quad_out_grad)
    trip_agg_grad = outer(trip_out_grad, trip_up_full).astype(BF16)
    quad_agg_grad = outer(quad_out_grad, quad_up_full).astype(BF16)
    proj_grad = inner(ends, message_grad)
    width = atom_low.shape[1]
    source_sums = inner(source_hot, message_grad).astype(BF16)
    target_sums = inner(target_hot, message_grad).astype(BF16)
    source_back = outer(source_sums, proj_full[:width])
    target_back = outer(target_sums, proj_full[width:])
    wide_atoms = source_back.reshape(3, atoms_here, width)
    wide_atoms = wide_atoms.at[1].add(target_back)

    def split(array, axis):
        return jnp.split(array, parts, axis=axis)

    def share(members):
        packed = [
            jnp.concatenate([member[i] for member in members], axis=0).astype(BF16)
            for i in range(parts)
        ]
        packed = reorder(packed, rank)
        got = chan_swap(jnp.stack([packed[1], packed[3]]), 1).astype(F32)
        mine = packed[0].astype(F32) + got[0]
        return mine, (packed[2].astype(F32) + got[1]).astype(BF16)

    mine, other = share(
        [
            split(trip_up_grad, 1),
            split(quad_up_grad, 1),
            split(proj_grad[:width], 1),
            split(proj_grad[width:], 1),
            split(resid_first_grad, 1),
            [columns(block) for block in split(resid_second_grad, 0)],
            [columns(block) for block in split(edge_to_atom_grad, 0)],
        ]
    )
    other_got = chan_swap(other, 2)
    atom_rows = jnp.concatenate(
        [columns(atom_update_grad), columns(output_first_grad)], axis=0
    ).astype(BF16)

    wide_low = wide_atoms.astype(BF16)
    wide_atoms = wide_atoms + chan_swap(wide_low, 1).astype(F32)
    wide_low = wide_atoms.astype(BF16)
    wide_atoms = wide_atoms + chan_swap(wide_low, 2).astype(F32)
    atom_grad = (
        atoms_new_grad
        + wide_atoms[1]
        + edge_shift(wide_atoms[0].astype(BF16), -1).astype(F32)
        + edge_shift(wide_atoms[2].astype(BF16), 1).astype(F32)
    )
    tag_table_grad = jnp.dot(tag_onehot.T, atom_grad, precision=HIGHEST)

    pieces = 3 * parts

    def fold_table(table):
        table = table.reshape(3, parts, -1, LANES)
        got = chan_swap(jnp.stack([table[:, 1], table[:, 3]]), 1).astype(F32)
        mine = table[:, 0].astype(F32) + got[0]
        return mine, (table[:, 2].astype(F32) + got[1]).astype(BF16)

    def return_table(mine):
        to_before = edge_shift(mine[0].astype(BF16), -1)
        to_after = edge_shift(mine[2].astype(BF16), 1)
        return mine[1] + to_before.astype(F32) + to_after.astype(F32)

    trip_table = branch_backward(
        after(trip_index, other), trip_basis, trip_agg_grad, trip_bil, pieces, "trip_scatter"
    )
    trip_mine, trip_other = fold_table(trip_table)
    trip_got = chan_swap(trip_other, 2)
    quad_table = branch_backward(
        after(quad_index, trip_other), quad_basis, quad_agg_grad, quad_bil, pieces, "quad_scatter"
    )
    trip_grad = return_table(trip_mine + trip_got.astype(F32))
    quad_mine, quad_other = fold_table(quad_table)
    quad_grad = return_table(quad_mine + chan_swap(quad_other, 2).astype(F32))
    branch_grad = jnp.concatenate(
        [unfold_lanes(trip_grad, trip_width), unfold_lanes(quad_grad, quad_width)], axis=1
    )
    down_grad = (branch_grad * radial_pre * silu_grad(down_pre)).astype(BF16)
    radial_grad = (branch_grad * jax.nn.silu(down_pre)).astype(BF16)
    down_weight_grad = inner(own_edges, down_grad)
    radial_weight_grad = inner(own_radial, radial_grad)

    def give_back(array):
        blocks = jnp.stack([array[:, i * cols : (i + 1) * cols] for i in range(parts)])
        return jnp.concatenate(exchange(blocks, rank), axis=0)

    edges_out = give_back(edges_low)
    one_out = give_back(one_grad.astype(BF16)).astype(F32)
    down_wire = jnp.concatenate(
        [fold_lanes(down_grad[:, :trip_width]), fold_lanes(down_grad[:, trip_width:])], axis=0
    )
    down_all = reorder(gather_chan(down_wire), rank)
    down_all = jnp.concatenate(
        [
            jnp.concatenate(
                [
                    unfold_lanes(block[:trip_rows], trip_width),
                    unfold_lanes(block[trip_rows:], quad_width),
                ],
                axis=1,
            )
            for block in down_all
        ],
        axis=0,
    )
    down_rows = lax.dynamic_slice_in_dim(down_full, rank * cols, cols, 0)
    edge_grad = one_out + outer(down_all, down_rows)

    mine = (mine + other_got.astype(F32)).astype(BF16)
    early = mine.shape[0]
    summed = edge_reduce(jnp.concatenate([mine, atom_rows], axis=0)).astype(F32)

    def ungroup(array, folds):
        groups, rows, out = array.shape
        array = array.reshape(groups, folds, rows // folds, out)
        return jnp.transpose(array, (1, 0, 2, 3)).reshape(groups * folds, rows // folds, out)

    trip_bilinear_grad = ungroup(
        jnp.einsum("gej,eo->gjo", trip_sum, trip_agg_grad, preferred_element_type=F32), trip_folds
    )
    quad_bilinear_grad = ungroup(
        jnp.einsum("gej,eo->gjo", quad_sum, quad_agg_grad, preferred_element_type=F32), quad_folds
    )
    small_grad = jnp.concatenate([down_weight_grad, radial_weight_grad], axis=0)
    late_mine, late_other = share(
        [
            [
                columns(jnp.concatenate([trip_block, quad_block], axis=1).T)
                for trip_block, quad_block in zip(
                    split(small_grad[:, :trip_width], 1), split(small_grad[:, trip_width:], 1)
                )
            ],
            [fold_lanes(block.reshape(-1, trip_out)) for block in split(trip_bilinear_grad, 1)],
            [fold_lanes(block.reshape(-1, quad_out)) for block in split(quad_bilinear_grad, 1)],
        ]
    )
    late = late_mine + chan_swap(late_other, 2).astype(F32)
    late = edge_sum(late, BF16)
    tiny = edge_sum(jnp.concatenate([output_second_grad[None], tag_table_grad], axis=0), F32)
    parts_out = [summed[offsets[i] : offsets[i + 1]] for i in range(len(sizes))]
    small_out = uncolumns(late[:small_rows], long).T
    trip_bil_out = late[small_rows : small_rows + trip_bil_rows]
    quad_bil_out = late[small_rows + trip_bil_rows :]
    atom_out = summed[early:]
    half = atom_out.shape[0] // 2
    return (
        edges_out,
        atoms_low,
        energy,
        edge_grad,
        atom_grad,
        small_out[:channels, :trip_cols],
        small_out[channels:, :trip_cols],
        unfold_lanes(trip_bil_out, trip_out).reshape(triplet_bilinear_weight.shape),
        parts_out[0],
        small_out[:channels, trip_cols:],
        small_out[channels:, trip_cols:],
        unfold_lanes(quad_bil_out, quad_out).reshape(quad_bilinear.shape),
        parts_out[1],
        parts_out[2],
        parts_out[3],
        parts_out[4],
        uncolumns(parts_out[5], resid_second.shape[1]),
        uncolumns(parts_out[6], edge_to_atom.shape[1]),
        uncolumns(atom_out[:half], atom_update.shape[1]),
        uncolumns(atom_out[half:], output_first.shape[1]),
        tiny[0],
        tiny[1:],
    )


def solution(mesh):
    return jax.shard_map(
        per_device,
        mesh=mesh,
        in_specs=(
            P("edge", "chan"),
            P("edge", None),
            P("edge", None),
            P(None, None, "edge"),
            P(None, None, "edge"),
            P("edge"),
            P("edge"),
            P("edge"),
            P(None, "edge"),
            P(None, "edge"),
            P(None, "edge"),
            P(None, "edge"),
            P(None, "chan"),
            P(None, "chan"),
            P(None, "chan", None),
            P(None, "chan"),
            P(None, "chan"),
            P(None, "chan"),
            P(None, "chan", None),
            P(None, "chan"),
            P(None, "chan"),
            P(None, "chan"),
            P(None, "chan"),
            P("chan", None),
            P("chan", None),
            P(),
            P(),
            P(),
            P(),
            P("edge", "chan"),
            P("edge", None),
            P("edge"),
        ),
        out_specs=(
            P("edge", "chan"),
            P("edge", None),
            P("edge"),
            P("edge", "chan"),
            P("edge", None),
            P(None, "chan"),
            P(None, "chan"),
            P(None, "chan", None),
            P(None, "chan"),
            P(None, "chan"),
            P(None, "chan"),
            P(None, "chan", None),
            P(None, "chan"),
            P(None, "chan"),
            P(None, "chan"),
            P(None, "chan"),
            P("chan", None),
            P("chan", None),
            P(),
            P(),
            P(),
            P(),
        ),
        check_vma=False,
    )
```

profile of v0, /device:TPU:0, one launch (start us, length us, event | category | flops | bytes accessed | tf_op | source)
XLA Modules:
  0.0 460.1 jit_solution(6747508351310696252)
XLA Ops:
  8.3 4.8 %collective-permute-start.15 = (bf16[128,256]{1,0:T(8,128)(2,1)S(1)}, bf16[128,256]{1,0:T(8,128)(2,1)S(1)}, u32[]{:S(2)}, u32[]{:S(2)}) collective-permute-start(bf16[128,256]{1,0:T(8,128)(2,1)S(1)} %get-tuple-element.411), channel_id=1, source_target_pairs={{0,28},{4,0},{8,4},{12,8},{16,12},{20,16},{24,20},{28,24},{1,29},{... | collective-permute-start | bytes 196616 | tf_op jit(solution)/shard_map/ppermute | solution.py:30
  34.8 4.9 %collective-permute-done.1 = bf16[1024,128]{1,0:T(8,128)(2,1)S(1)} collective-permute-done((bf16[1024,128]{1,0:T(8,128)(2,1)S(1)}, bf16[1024,128]{1,0:T(8,128)(2,1)S(1)}, u32[]{:S(2)}, u32[]{:S(2)}) %collective-permute-start.1) | collective-permute-done | bytes 262176 | tf_op jit(solution)/shard_map/ppermute | solution.py:20
  39.7 4.5 collective-permute-done
  46.3 4.8 %collective-permute-start.7 = (bf16[768,128]{1,0:T(8,128)(2,1)S(1)}, bf16[768,128]{1,0:T(8,128)(2,1)S(1)}, u32[]{:S(2)}, u32[]{:S(2)}) collective-permute-start(bf16[768,128]{1,0:T(8,128)(2,1)S(1)} %maximum_maximum_fusion.2), channel_id=1, source_target_pairs={{0,28},{4,0},{8,4},{12,8},{16,12},{20,16},{24,20},{28,24},{1,29},{... | collective-permute-start | bytes 589832 | tf_op jit(solution)/shard_map/ppermute | solution.py:30
  51.3 4.4 collective-permute-done.7
  55.7 5.1 %collective-permute-done.6 = bf16[768,128]{1,0:T(8,128)(2,1)S(1)} collective-permute-done((bf16[768,128]{1,0:T(8,128)(2,1)S(1)}, bf16[768,128]{1,0:T(8,128)(2,1)S(1)}, u32[]{:S(2)}, u32[]{:S(2)}) %collective-permute-start.6) | collective-permute-done | bytes 196640 | tf_op jit(solution)/shard_map/ppermute | solution.py:30
  66.5 6.5 %collective-permute-done.8 = bf16[2,768,128]{2,1,0:T(8,128)(2,1)S(1)} collective-permute-done((bf16[2,768,128]{2,1,0:T(8,128)(2,1)S(1)}, bf16[2,768,128]{2,1,0:T(8,128)(2,1)S(1)}, u32[]{:S(2)}, u32[]{:S(2)}) %collective-permute-start.8) | collective-permute-done | bytes 393248 | tf_op jit(solution)/shard_map/ppermute | solution.py:20
  85.3 5.6 %reshape.1506 = bf16[16,16,64,16]{3,2,1,0:T(8,128)(2,1)} reshape(bf16[16,16,1024]{2,1,0:T(8,128)(2,1)} %dynamic-slice_multiply_fusion.1) | data formatting | bytes 1048576 | tf_op jit(solution)/shard_map/reshape | solution.py:321
  90.9 3.6 copy.319
  109.7 18.7 %quad_gather.1 = (bf16[1024,32]{1,0:T(8,128)(2,1)}, bf16[8,1024,128]{2,1,0:T(8,128)(2,1)}) custom-call(s32[8192]{0:T(1024)} %bitcast.663, bf16[12,256,128]{2,1,0:T(8,128)(2,1)} %slice.1716.packed_ref, bf16[64,32,128]{2,1,0:T(8,128)(2,1)} %copy.325.basis_ref, bf16[8,128,32]{2,1,0:T(8,128)(2,1)} %bitcast.626), custom_call_target="tpu_custom_call" | custom-call | flops 20000000000 | bytes 10000000 | tf_op jit(solution)/shard_map/quad_gather/pallas_call | solution.py:177
  128.4 27.5 %trip_gather.1 = (bf16[1024,64]{1,0:T(8,128)(2,1)}, bf16[8,1024,128]{2,1,0:T(8,128)(2,1)}) custom-call(s32[16384]{0:T(1024)} %bitcast.661, bf16[12,512,128]{2,1,0:T(8,128)(2,1)} %slice.1701.packed_ref, bf16[64,16,256]{2,1,0:T(8,128)(2,1)} %copy.321.basis_ref, bf16[8,128,64]{2,1,0:T(8,128)(2,1)} %bitcast.628), custom_call_target="tpu_custom_call" | custom-call | flops 20000000000 | bytes 10000000 | tf_op jit(solution)/shard_map/trip_gather/pallas_call | solution.py:177
  177.5 5.9 %collective-permute-done.17 = bf16[1024,128]{1,0:T(8,128)(2,1)S(1)} collective-permute-done((bf16[1024,128]{1,0:T(8,128)(2,1)S(1)}, bf16[1024,128]{1,0:T(8,128)(2,1)S(1)}, u32[]{:S(2)}, u32[]{:S(2)}) %collective-permute-start.17) | collective-permute-done | bytes 262176 | tf_op jit(solution)/shard_map/ppermute | solution.py:20
  183.4 4.1 collective-permute-done.16
  206.3 4.1 multiply_convert_fusion
  243.2 13.8 %collective-permute-done.39 = bf16[3,128,256]{2,1,0:T(8,128)(2,1)S(1)} collective-permute-done((bf16[3,128,256]{2,1,0:T(8,128)(2,1)S(1)}, bf16[3,128,256]{2,1,0:T(8,128)(2,1)S(1)}, u32[]{:S(2)}, u32[]{:S(2)}) %collective-permute-start.39) | collective-permute-done | bytes 196640 | tf_op jit(solution)/shard_map/ppermute | solution.py:20
  261.5 4.6 collective-permute-done.41
  266.6 3.6 collective-permute-done.54
  275.5 32.9 %trip_scatter.1 = bf16[12,512,128]{2,1,0:T(8,128)(2,1)} custom-call(s32[16384]{0:T(1024)} %bitcast.662, bf16[64,16,256]{2,1,0:T(8,128)(2,1)} %copy.321.basis_ref, bf16[1024,64]{1,0:T(8,128)(2,1)} %copy-done.61, bf16[8,128,64]{2,1,0:T(8,128)(2,1)} %bitcast.629), custom_call_target="tpu_custom_call" | custom-call | flops 20000000000 | bytes 10000000 | tf_op jit(solution)/shard_map/trip_scatter/pallas_call | solution.py:276
  314.2 24.6 %quad_scatter.1 = bf16[12,256,128]{2,1,0:T(8,128)(2,1)} custom-call(s32[8192]{0:T(1024)} %bitcast.664, bf16[64,32,128]{2,1,0:T(8,128)(2,1)} %copy.325.basis_ref, bf16[1024,32]{1,0:T(8,128)(2,1)} %convolution_convert_fusion.2.grad_ref, bf16[8,128,32]{2,1,0:T(8,128)(2,1)} %bitcast.627), custom_call_target="tpu_custom_call" | custom-call | flops 20000000000 | bytes 10000000 | tf_op jit(solution)/shard_map/quad_scatter/pallas_call | solution.py:276
  359.8 6.7 %collective-permute-done.29 = bf16[3,512,128]{2,1,0:T(8,128)(2,1)} collective-permute-done((bf16[3,512,128]{2,1,0:T(8,128)(2,1)}, bf16[3,512,128]{2,1,0:T(8,128)(2,1)}, u32[]{:S(2)}, u32[]{:S(2)}) %collective-permute-start.29) | collective-permute-done | bytes 393248 | tf_op jit(solution)/shard_map/ppermute | solution.py:20
  373.9 5.2 %collective-permute-done.31 = bf16[512,128]{1,0:T(8,128)(2,1)S(1)} collective-permute-done((bf16[512,128]{1,0:T(8,128)(2,1)S(1)}, bf16[512,128]{1,0:T(8,128)(2,1)S(1)}, u32[]{:S(2)}, u32[]{:S(2)}) %collective-permute-start.31) | collective-permute-done | bytes 131104 | tf_op jit(solution)/shard_map/ppermute | solution.py:30
  397.1 3.9 collective-permute-done.36
  407.6 6.4 %collective-permute-done.46 = bf16[312,128]{1,0:T(8,128)(2,1)S(1)} collective-permute-done((bf16[312,128]{1,0:T(8,128)(2,1)S(1)}, bf16[312,128]{1,0:T(8,128)(2,1)S(1)}, u32[]{:S(2)}, u32[]{:S(2)}) %collective-permute-start.46) | collective-permute-done | bytes 79904 | tf_op jit(solution)/shard_map/ppermute | solution.py:25
  419.3 40.4 %convert_add_fusion = f32[4096,128]{1,0:T(8,128)} fusion(bf16[1024,128]{1,0:T(8,128)(2,1)S(1)} %copy-done.60, bf16[1024,128]{1,0:T(8,128)(2,1)S(1)} %copy-done.59, bf16[1024,128]{1,0:T(8,128)(2,1)S(1)} %copy-done.58, bf16[1024,128]{1,0:T(8,128)(2,1)S(1)} %copy-done.57, bf16[256,32]{1,0:T(8,128)(2,1)S(1)} %get-tuple-element.341, ...), kind=kOutput, calls=%fused_computation.3 | convolution fusion | flops 124256256 | bytes 3956740 | tf_op jit(solution)/shard_map/dot_general | solution.py:81
  (816 shorter events, 208.9 us)
Async XLA Ops:
  3.4 30.1 %collective-permute-start.5 = (bf16[312,128]{1,0:T(8,128)(2,1)S(1)}, bf16[312,128]{1,0:T(8,128)(2,1)S(1)}, u32[]{:S(2)}, u32[]{:S(2)}) collective-permute-start(bf16[312,128]{1,0:T(8,128)(2,1)S(1)} %constant_dynamic-update-slice_fusion), channel_id=1, source_target_pairs={{0,1},{1,0},{2,3},{3,2},{4,5},{5,4},{6,7},{7,6},{8,9},{9,8},{10,11... | collective-permute-start | bytes 239624 | tf_op jit(solution)/shard_map/ppermute | solution.py:20
  4.0 29.8 %collective-permute-start.4 = (bf16[312,128]{1,0:T(8,128)(2,1)S(1)}, bf16[312,128]{1,0:T(8,128)(2,1)S(1)}, u32[]{:S(2)}, u32[]{:S(2)}) collective-permute-start(bf16[312,128]{1,0:T(8,128)(2,1)S(1)} %constant_dynamic-update-slice_fusion), channel_id=1, source_target_pairs={{0,2},{1,3},{2,0},{3,1},{4,6},{5,7},{6,4},{7,5},{8,10},{9,11},{10,... | collective-permute-start | bytes 239624 | tf_op jit(solution)/shard_map/ppermute | solution.py:20
  6.6 27.2 %collective-permute-start.3 = (bf16[312,128]{1,0:T(8,128)(2,1)S(1)}, bf16[312,128]{1,0:T(8,128)(2,1)S(1)}, u32[]{:S(2)}, u32[]{:S(2)}) collective-permute-start(bf16[312,128]{1,0:T(8,128)(2,1)S(1)} %constant_dynamic-update-slice_fusion), channel_id=1, source_target_pairs={{0,3},{1,2},{2,1},{3,0},{4,7},{5,6},{6,5},{7,4},{8,11},{9,10},{10,... | collective-permute-start | bytes 239624 | tf_op jit(solution)/shard_map/ppermute | solution.py:20
  8.3 22.1 %collective-permute-start.15 = (bf16[128,256]{1,0:T(8,128)(2,1)S(1)}, bf16[128,256]{1,0:T(8,128)(2,1)S(1)}, u32[]{:S(2)}, u32[]{:S(2)}) collective-permute-start(bf16[128,256]{1,0:T(8,128)(2,1)S(1)} %get-tuple-element.411), channel_id=1, source_target_pairs={{0,28},{4,0},{8,4},{12,8},{16,12},{20,16},{24,20},{28,24},{1,29},{... | collective-permute-start | bytes 196616 | tf_op jit(solution)/shard_map/ppermute | solution.py:30
  13.1 17.4 %collective-permute-start.14 = (bf16[128,256]{1,0:T(8,128)(2,1)S(1)}, bf16[128,256]{1,0:T(8,128)(2,1)S(1)}, u32[]{:S(2)}, u32[]{:S(2)}) collective-permute-start(bf16[128,256]{1,0:T(8,128)(2,1)S(1)} %get-tuple-element.411), channel_id=1, source_target_pairs={{0,4},{4,8},{8,12},{12,16},{16,20},{20,24},{24,28},{28,0},{1,5},{5... | collective-permute-start | bytes 196616 | tf_op jit(solution)/shard_map/ppermute | solution.py:30
  64.0 32.2 %collective-permute-start.10 = (bf16[768,128]{1,0:T(8,128)(2,1)S(1)}, bf16[768,128]{1,0:T(8,128)(2,1)}, u32[]{:S(2)}, u32[]{:S(2)}) collective-permute-start(bf16[768,128]{1,0:T(8,128)(2,1)S(1)} %maximum_maximum_fusion.2), channel_id=1, source_target_pairs={{0,2},{1,3},{2,0},{3,1},{4,6},{5,7},{6,4},{7,5},{8,10},{9,11},{10,... | collective-permute-start | bytes 589832 | tf_op jit(solution)/shard_map/ppermute | solution.py:20
  72.9 25.7 %collective-permute-start.12 = (bf16[1888,128]{1,0:T(8,128)(2,1)}, bf16[1888,128]{1,0:T(8,128)(2,1)}, u32[]{:S(2)}, u32[]{:S(2)}) collective-permute-start(bf16[1888,128]{1,0:T(8,128)(2,1)} %constant_dynamic-update-slice_fusion.39), channel_id=1, source_target_pairs={{0,2},{1,3},{2,0},{3,1},{4,6},{5,7},{6,4},{7,5},{8,10},{9,11},{10,... | collective-permute-start | bytes 1449992 | tf_op jit(solution)/shard_map/ppermute | solution.py:20
  75.4 26.6 %collective-permute-start.9 = (bf16[2,2,768,128]{3,2,1,0:T(8,128)(2,1)}, bf16[2,2,768,128]{3,2,1,0:T(8,128)(2,1)}, u32[]{:S(2)}, u32[]{:S(2)}) collective-permute-start(bf16[2,2,768,128]{3,2,1,0:T(8,128)(2,1)} %pad_maximum_fusion.8), channel_id=1, source_target_pairs={{0,1},{1,0},{2,3},{3,2},{4,5},{5,4},{6,7},{7,6},{8,9},{9,8},{10,11... | collective-permute-start | bytes 2359304 | tf_op jit(solution)/shard_map/ppermute | solution.py:20
  98.8 75.5 %collective-permute-start.23 = (bf16[1024,128]{1,0:T(8,128)(2,1)S(1)}, bf16[1024,128]{1,0:T(8,128)(2,1)S(1)}, u32[]{:S(2)}, u32[]{:S(2)}) collective-permute-start(bf16[1024,128]{1,0:T(8,128)(2,1)S(1)} %get-tuple-element.139), channel_id=1, source_target_pairs={{0,1},{1,0},{2,3},{3,2},{4,5},{5,4},{6,7},{7,6},{8,9},{9,8},{10,11... | collective-permute-start | bytes 786440 | tf_op jit(solution)/shard_map/ppermute | solution.py:20
  98.9 75.9 %collective-permute-start.22 = (bf16[1024,128]{1,0:T(8,128)(2,1)S(1)}, bf16[1024,128]{1,0:T(8,128)(2,1)S(1)}, u32[]{:S(2)}, u32[]{:S(2)}) collective-permute-start(bf16[1024,128]{1,0:T(8,128)(2,1)S(1)} %get-tuple-element.140), channel_id=1, source_target_pairs={{0,2},{1,3},{2,0},{3,1},{4,6},{5,7},{6,4},{7,5},{8,10},{9,11},{10,... | collective-permute-start | bytes 786440 | tf_op jit(solution)/shard_map/ppermute | solution.py:20
  99.4 76.4 %collective-permute-start.21 = (bf16[1024,128]{1,0:T(8,128)(2,1)S(1)}, bf16[1024,128]{1,0:T(8,128)(2,1)S(1)}, u32[]{:S(2)}, u32[]{:S(2)}) collective-permute-start(bf16[1024,128]{1,0:T(8,128)(2,1)S(1)} %get-tuple-element.141), channel_id=1, source_target_pairs={{0,3},{1,2},{2,1},{3,0},{4,7},{5,6},{6,5},{7,4},{8,11},{9,10},{10,... | collective-permute-start | bytes 786440 | tf_op jit(solution)/shard_map/ppermute | solution.py:20
  102.0 53.9 %collective-permute-start.13 = (bf16[2,1888,128]{2,1,0:T(8,128)(2,1)S(1)}, bf16[2,1888,128]{2,1,0:T(8,128)(2,1)S(1)}, u32[]{:S(2)}, u32[]{:S(2)}) collective-permute-start(bf16[2,1888,128]{2,1,0:T(8,128)(2,1)S(1)} %pad_maximum_fusion.6), channel_id=1, source_target_pairs={{0,1},{1,0},{2,3},{3,2},{4,5},{5,4},{6,7},{7,6},{8,9},{9,8},{10,11... | collective-permute-start | bytes 2899976 | tf_op jit(solution)/shard_map/ppermute | solution.py:20
  174.8 12.7 %collective-permute-start.16 = (bf16[1024,128]{1,0:T(8,128)(2,1)S(1)}, bf16[1024,128]{1,0:T(8,128)(2,1)S(1)}, u32[]{:S(2)}, u32[]{:S(2)}) collective-permute-start(bf16[1024,128]{1,0:T(8,128)(2,1)S(1)} %get-tuple-element.144), channel_id=1, source_target_pairs={{0,3},{1,2},{2,1},{3,0},{4,7},{5,6},{6,5},{7,4},{8,11},{9,10},{10,... | collective-permute-start | bytes 786440 | tf_op jit(solution)/shard_map/ppermute | solution.py:20
  176.9 14.2 %collective-permute-start.20 = (f32[128,256]{1,0:T(8,128)S(1)}, f32[128,256]{1,0:T(8,128)S(1)}, u32[]{:S(2)}, u32[]{:S(2)}) collective-permute-start(f32[128,256]{1,0:T(8,128)S(1)} %add.309), channel_id=1, source_target_pairs={{0,2},{1,3},{2,0},{3,1},{4,6},{5,7},{6,4},{7,5},{8,10},{9,11},{10,... | collective-permute-start | bytes 393224 | tf_op jit(solution)/shard_map/ppermute | solution.py:20
  238.3 109.7 %collective-permute-start.26 = (bf16[1024,128]{1,0:T(8,128)(2,1)}, bf16[1024,128]{1,0:T(8,128)(2,1)}, u32[]{:S(2)}, u32[]{:S(2)}) collective-permute-start(bf16[1024,128]{1,0:T(8,128)(2,1)} %get-tuple-element.132), channel_id=1, source_target_pairs={{0,1},{1,0},{2,3},{3,2},{4,5},{5,4},{6,7},{7,6},{8,9},{9,8},{10,11... | collective-permute-start | bytes 786440 | tf_op jit(solution)/shard_map/ppermute | solution.py:20
  238.7 112.0 %collective-permute-start.25 = (bf16[1024,128]{1,0:T(8,128)(2,1)}, bf16[1024,128]{1,0:T(8,128)(2,1)}, u32[]{:S(2)}, u32[]{:S(2)}) collective-permute-start(bf16[1024,128]{1,0:T(8,128)(2,1)} %get-tuple-element.133), channel_id=1, source_target_pairs={{0,2},{1,3},{2,0},{3,1},{4,6},{5,7},{6,4},{7,5},{8,10},{9,11},{10,... | collective-permute-start | bytes 786440 | tf_op jit(solution)/shard_map/ppermute | solution.py:20
  239.2 111.5 %collective-permute-start.24 = (bf16[1024,128]{1,0:T(8,128)(2,1)}, bf16[1024,128]{1,0:T(8,128)(2,1)}, u32[]{:S(2)}, u32[]{:S(2)}) collective-permute-start(bf16[1024,128]{1,0:T(8,128)(2,1)} %get-tuple-element.134), channel_id=1, source_target_pairs={{0,3},{1,2},{2,1},{3,0},{4,7},{5,6},{6,5},{7,4},{8,11},{9,10},{10,... | collective-permute-start | bytes 786440 | tf_op jit(solution)/shard_map/ppermute | solution.py:20
  242.5 14.6 %collective-permute-start.39 = (bf16[3,128,256]{2,1,0:T(8,128)(2,1)S(1)}, bf16[3,128,256]{2,1,0:T(8,128)(2,1)S(1)}, u32[]{:S(2)}, u32[]{:S(2)}) collective-permute-start(bf16[3,128,256]{2,1,0:T(8,128)(2,1)S(1)} %fusion.97), channel_id=1, source_target_pairs={{0,2},{1,3},{2,0},{3,1},{4,6},{5,7},{6,4},{7,5},{8,10},{9,11},{10,... | collective-permute-start | bytes 589832 | tf_op jit(solution)/shard_map/ppermute | solution.py:20
  273.8 79.2 %collective-permute-start.56 = (f32[4,256]{1,0:T(4,128)S(1)}, f32[4,256]{1,0:T(4,128)S(1)}, u32[]{:S(2)}, u32[]{:S(2)}) collective-permute-start(f32[4,256]{1,0:T(4,128)S(1)} %add.357), channel_id=1, source_target_pairs={{0,16},{4,20},{8,24},{12,28},{16,0},{20,4},{24,8},{28,12},{1,17},{... | collective-permute-start | bytes 12296 | tf_op jit(solution)/shard_map/ppermute | solution.py:25
  275.0 34.9 %collective-permute-start.47 = (bf16[1888,128]{1,0:T(8,128)(2,1)}, bf16[1888,128]{1,0:T(8,128)(2,1)}, u32[]{:S(2)}, u32[]{:S(2)}) collective-permute-start(bf16[1888,128]{1,0:T(8,128)(2,1)} %fusion.61), channel_id=1, source_target_pairs={{0,2},{1,3},{2,0},{3,1},{4,6},{5,7},{6,4},{7,5},{8,10},{9,11},{10,... | collective-permute-start | bytes 1449992 | tf_op jit(solution)/shard_map/ppermute | solution.py:20
  312.2 26.5 %collective-permute-start.48 = (bf16[1472,128]{1,0:T(8,128)(2,1)S(1)}, bf16[1472,128]{1,0:T(8,128)(2,1)S(1)}, u32[]{:S(2)}, u32[]{:S(2)}) collective-permute-start(bf16[1472,128]{1,0:T(8,128)(2,1)S(1)} %broadcast_select_fusion.16), channel_id=1, source_target_pairs={{0,4},{4,0},{8,12},{12,8},{16,20},{20,16},{24,28},{28,24},{1,5},{5... | collective-permute-start | bytes 1130504 | tf_op jit(solution)/shard_map/ppermute | solution.py:25
  359.2 20.1 %collective-permute-start.33 = (bf16[3,256,128]{1,2,0:T(8,128)(2,1)S(1)}, bf16[3,256,128]{1,2,0:T(8,128)(2,1)S(1)}, u32[]{:S(2)}, u32[]{:S(2)}) collective-permute-start(bf16[3,256,128]{1,2,0:T(8,128)(2,1)S(1)} %fusion.94), channel_id=1, source_target_pairs={{0,2},{1,3},{2,0},{3,1},{4,6},{5,7},{6,4},{7,5},{8,10},{9,11},{10,... | collective-permute-start | bytes 589832 | tf_op jit(solution)/shard_map/ppermute | solution.py:20
  382.4 19.2 %collective-permute-start.53 = (bf16[1472,128]{1,0:T(8,128)(2,1)}, bf16[1472,128]{1,0:T(8,128)(2,1)S(1)}, u32[]{:S(2)}, u32[]{:S(2)}) collective-permute-start(bf16[1472,128]{1,0:T(8,128)(2,1)} %pad_maximum_fusion.19), channel_id=1, source_target_pairs={{0,4},{4,0},{8,12},{12,8},{16,20},{20,16},{24,28},{28,24},{1,5},{5... | collective-permute-start | bytes 1130504 | tf_op jit(solution)/shard_map/ppermute | solution.py:25
  401.0 17.0 %collective-permute-start.37 = (bf16[2,768,128]{2,1,0:T(8,128)(2,1)S(1)}, bf16[2,768,128]{2,1,0:T(8,128)(2,1)S(1)}, u32[]{:S(2)}, u32[]{:S(2)}) collective-permute-start(bf16[2,768,128]{2,1,0:T(8,128)(2,1)S(1)} %pad_maximum_fusion.18), channel_id=1, source_target_pairs={{0,1},{1,0},{2,3},{3,2},{4,5},{5,4},{6,7},{7,6},{8,9},{9,8},{10,11... | collective-permute-start | bytes 1179656 | tf_op jit(solution)/shard_map/ppermute | solution.py:20
  (213 other events, 1252.8 us)
where the time goes:
time: 466 us; the launch traced here: 460 us
  Pallas kernels  104 us (22%)
  waiting for transfers between devices  98.5 us (21%)
  matrix products  91.1 us (20%)
  local copies, waits for them, and re-layouts  77.7 us (17%)
  starting transfers between devices  43.9 us (9%)
  other arithmetic  40.5 us (9%)
  between operations  4.76 us (1%)
    dot_general x9, matrix products, outer(): lax.dot_general(first_op, second_op, (((1,), (1,)), ((), ())), preferred_...  58.2 us
    pallas_call x2, Pallas kernels, branch_backward(): pl.pallas_call(functools.partial(scatter_body, folds=folds), out_shape=ja...  57.5 us
    ppermute x35, waiting for transfers between devices, chan_swap(): return lax.ppermute(value, 'chan', [(i, i ^ mask) for i in range(count)])  56.9 us
    pallas_call x2, Pallas kernels, branch_forward(): pl.pallas_call(functools.partial(gather_body, folds=folds), out_shape=(ja...  46.2 us
    unnamed x479, local copies, waits for them, and re-layouts  31.2 us
    ppermute x10, waiting for transfers between devices, edge_shift(): lax.ppermute(value, 'edge', [(i, (i + step) % count) for i in range(count)])  27.7 us
    ppermute x35, starting transfers between devices, chan_swap(): return lax.ppermute(value, 'chan', [(i, i ^ mask) for i in range(count)])  21.9 us
    dot_general x15, matrix products, matmul(): return jnp.dot(first_op, second_op, preferred_element_type=F32)  18.4 us
  transfers between devices with their start and end apart: 57, of which 24 were waited for; matrix products, arithmetic and copies ran while one was open for 25% of the time, Pallas kernels for 23%

commit v1 on v0

--- a/solution.py
+++ b/solution.py
@@ -34,6 +34,10 @@
     return lax.optimization_barrier((value,) + others)[0]
 
 
+def gate(values, *others):
+    return list(lax.optimization_barrier(tuple(values) + others)[: len(values)])
+
+
 def gather_direct(value):
     return [value] + [chan_swap(value, step) for step in (1, 2, 3)]
 
@@ -104,34 +108,34 @@
     return jnp.concatenate(masked, axis=0)
 
 
-def gather_body(
-    index_ref, packed_ref, basis_ref, bilinear_ref, agg_ref, sum_ref, table, rows_a, rows_b, *, folds
-):
-    pieces, piece_rows, _ = packed_ref.shape
+def gather_body(index_ref, basis_ref, bilinear_ref, *refs, folds, first_row):
+    packed_refs = refs[:-5]
+    agg_ref, sum_ref, table, rows_a, rows_b = refs[-5:]
     groups, edges, _ = sum_ref.shape
     basis_count = groups * folds
     width = LANES // folds
+    piece_rows = edges // folds
     slots = basis_ref.shape[2] // BLOCK
     step = min(piece_rows, 128)
-    per_piece = piece_rows // step
     lane = lax.broadcasted_iota(jnp.int32, (step, LANES), 1) // width
 
-    def unpack(turn, _):
-        piece = turn // per_piece
-        start = pl.multiple_of((turn % per_piece) * step, step)
-        values = packed_ref[piece, pl.ds(start, step), :].astype(F32)
-        turned = [values] + [
-            pltpu.roll(values, shift * width, 1) for shift in range(1, folds)
-        ]
-        for fold in range(folds):
-            place = pl.multiple_of((piece * folds + fold) * piece_rows + start, step)
-            spread = turned[(0 - fold) % folds]
-            for group in range(1, folds):
-                spread = jnp.where(lane == group, turned[(group - fold) % folds], spread)
-            table[pl.ds(place, step), :] = spread
-        return 0
-
-    lax.fori_loop(0, pieces * per_piece, unpack, 0)
+    for piece, packed_ref in enumerate(packed_refs):
+
+        def unpack(turn, _, piece=piece, packed_ref=packed_ref):
+            start = pl.multiple_of(turn * step, step)
+            values = packed_ref[pl.ds(first_row + start, step), :].astype(F32)
+            turned = [values] + [
+                pltpu.roll(values, shift * width, 1) for shift in range(1, folds)
+            ]
+            for fold in range(folds):
+                place = pl.multiple_of((piece * folds + fold) * piece_rows + start, step)
+                spread = turned[(0 - fold) % folds]
+                for group in range(1, folds):
+                    spread = jnp.where(lane == group, turned[(group - fold) % folds], spread)
+                table[pl.ds(place, step), :] = spread
+            return 0
+
+        lax.fori_loop(0, piece_rows // step, unpack, 0)
     diagonal = diagonal_mask(basis_count * BLOCK, slots * BLOCK)
 
     def fetch(block, rows):
@@ -169,37 +173,100 @@
     agg_ref[...] = total.astype(BF16)
 
 
-def branch_forward(index, packed, basis, bilinear, name):
+def branch_forward(index, packed, first_row, basis, bilinear, name):
     groups, _, out_width = bilinear.shape
     edges = basis.shape[0] * BLOCK
     folds = basis.shape[1] // groups
     vmem = pl.BlockSpec(memory_space=pltpu.VMEM)
     return pl.pallas_call(
-        functools.partial(gather_body, folds=folds),
+        functools.partial(gather_body, folds=folds, first_row=first_row),
         out_shape=(
             jax.ShapeDtypeStruct((edges, out_width), BF16),
             jax.ShapeDtypeStruct((groups, edges, LANES), BF16),
         ),
-        in_specs=[pl.BlockSpec(memory_space=pltpu.SMEM), vmem, vmem, vmem],
+        in_specs=[pl.BlockSpec(memory_space=pltpu.SMEM)] + [vmem] * (2 + len(packed)),
         out_specs=(vmem, vmem),
         scratch_shapes=[
-            pltpu.VMEM((packed.shape[0] * edges, LANES), F32),
+            pltpu.VMEM((len(packed) * edges, LANES), F32),
             pltpu.VMEM((basis.shape[2], LANES), F32),
             pltpu.VMEM((basis.shape[2], LANES), F32),
         ],
         compiler_params=pltpu.CompilerParams(vmem_limit_bytes=56 << 20),
         cost_estimate=pl.CostEstimate(flops=20 * 10**9, transcendentals=0, bytes_accessed=10**7),
         name=name,
-    )(index, packed, basis, bilinear)
+    )(index, basis, bilinear, *packed)
+
+
+def basis_body(rank_ref, trip_vals, trip_keep, quad_vals, quad_keep, trip_ref, quad_ref, trip_rows, quad_rows):
+    del rank_ref
+    tile_slots = LANES // BLOCK
+
+    def build(vals_ref, keep_ref, out_ref, rows):
+        count, slots, _ = vals_ref.shape
+        vals = vals_ref[...].astype(F32) * keep_ref[...].astype(F32)[None]
+        rows[...] = vals.reshape(count * slots, LANES)
+        group = lax.broadcasted_iota(jnp.int32, (count, LANES), 1) // BLOCK
+        for tile in range(slots // tile_slots):
+            by_slot = [
+                rows[pl.ds(tile * tile_slots + slot, count, stride=slots), :]
+                for slot in range(tile_slots)
+            ]
+            for block in range(tile_slots):
+                joined = None
+                for slot, value in enumerate(by_slot):
+                    shift = (slot - block) * BLOCK % LANES
+                    turned = pltpu.roll(value, shift, 1) if shift else value
+                    joined = turned if joined is None else jnp.where(group == slot, turned, joined)
+                out_ref[block, :, tile * LANES : (tile + 1) * LANES] = joined.astype(BF16)
+
+    build(trip_vals, trip_keep, trip_ref, trip_rows)
+    build(quad_vals, quad_keep, quad_ref, quad_rows)
+
+
+def slot_basis(rank, circular, trip_mask, spherical, quad_mask, edges):
+    steps = edges // LANES
+    blocks = LANES // BLOCK
+
+    def source(array):
+        shape = array.shape[:-1] + (LANES,)
+        lead = (0,) * (len(shape) - 1)
+        return pl.BlockSpec(shape, lambda step, rank_ref: lead + (rank_ref[0] * steps + step,))
+
+    def target(count, slots):
+        return pl.BlockSpec((blocks, count, slots * BLOCK), lambda step, rank_ref: (step, 0, 0))
+
+    def shape_of(array):
+        count, slots, _ = array.shape
+        return jax.ShapeDtypeStruct((edges // BLOCK, count, slots * BLOCK), BF16)
+
+    def rows_of(array):
+        return pltpu.VMEM((array.shape[0] * array.shape[1], LANES), F32)
+
+    return pl.pallas_call(
+        basis_body,
+        grid_spec=pltpu.PrefetchScalarGridSpec(
+            num_scalar_prefetch=1,
+            grid=(steps,),
+            in_specs=[source(circular), source(trip_mask), source(spherical), source(quad_mask)],
+            out_specs=[target(*circular.shape[:2]), target(*spherical.shape[:2])],
+            scratch_shapes=[rows_of(circular), rows_of(spherical)],
+        ),
+        out_shape=(shape_of(circular), shape_of(spherical)),
+        cost_estimate=pl.CostEstimate(flops=10 * 10**9, transcendentals=0, bytes_accessed=10**7),
+        name="slot_basis",
+    )(rank[None], circular, trip_mask, spherical, quad_mask)
 
 
 TABLES = 4
 
 
 def scatter_body(
-    index_ref, basis_ref, grad_ref, bilinear_ref, packed_ref, part, rows_a, rows_b, *tables, folds
+    index_ref, basis_ref, grad_ref, bilinear_ref, *refs, folds, owners
 ):
-    pieces, piece_rows, _ = packed_ref.shape
+    packed_refs = refs[:owners]
+    part, rows_a, rows_b = refs[owners : owners + 3]
+    tables = refs[owners + 3 :]
+    sides, piece_rows, _ = packed_refs[0].shape
     groups, edges, _ = part.shape
     basis_count = groups * folds
     width = LANES // folds
@@ -248,42 +315,46 @@
     per_piece = piece_rows // step
     lane = lax.broadcasted_iota(jnp.int32, (step, LANES), 1) // width
 
-    def pack(turn, _):
-        piece = turn // per_piece
-        start = pl.multiple_of((turn % per_piece) * step, step)
-        joined = jnp.zeros((step, LANES), F32)
-        for fold in range(folds):
-            place = pl.multiple_of((piece * folds + fold) * piece_rows + start, step)
-            total = tables[0][pl.ds(place, step), :]
-            for table in tables[1:]:
-                total = total + table[pl.ds(place, step), :]
-            shift = LANES // 2
-            while shift >= width:
-                total = total + pltpu.roll(total, shift, 1)
-                shift //= 2
-            joined = jnp.where(lane == fold, total, joined)
-        packed_ref[piece, pl.ds(start, step), :] = joined.astype(BF16)
-        return 0
-
-    lax.fori_loop(0, pieces * per_piece, pack, 0)
-
-
-def branch_backward(index, basis, grad, bilinear, pieces, name):
+    for owner, packed_ref in enumerate(packed_refs):
+
+        def pack(turn, _, owner=owner, packed_ref=packed_ref):
+            side = turn // per_piece
+            piece = side * owners + owner
+            start = pl.multiple_of((turn % per_piece) * step, step)
+            joined = jnp.zeros((step, LANES), F32)
+            for fold in range(folds):
+                place = pl.multiple_of((piece * folds + fold) * piece_rows + start, step)
+                total = tables[0][pl.ds(place, step), :]
+                for table in tables[1:]:
+                    total = total + table[pl.ds(place, step), :]
+                shift = LANES // 2
+                while shift >= width:
+                    total = total + pltpu.roll(total, shift, 1)
+                    shift //= 2
+                joined = jnp.where(lane == fold, total, joined)
+            packed_ref[side, pl.ds(start, step), :] = joined.astype(BF16)
+            return 0
+
+        lax.fori_loop(0, sides * per_piece, pack, 0)
+
+
+def branch_backward(index, basis, grad, bilinear, sides, owners, name):
     edges = grad.shape[0]
     groups = bilinear.shape[0]
     folds = basis.shape[1] // groups
     vmem = pl.BlockSpec(memory_space=pltpu.VMEM)
+    out = jax.ShapeDtypeStruct((sides, edges // folds, LANES), BF16)
     return pl.pallas_call(
-        functools.partial(scatter_body, folds=folds),
-        out_shape=jax.ShapeDtypeStruct((pieces, edges // folds, LANES), BF16),
+        functools.partial(scatter_body, folds=folds, owners=owners),
+        out_shape=(out,) * owners,
         in_specs=[pl.BlockSpec(memory_space=pltpu.SMEM), vmem, vmem, vmem],
-        out_specs=vmem,
+        out_specs=(vmem,) * owners,
         scratch_shapes=[
             pltpu.VMEM((groups, edges, LANES), BF16),
             pltpu.VMEM((basis.shape[2], LANES), F32),
             pltpu.VMEM((basis.shape[2], LANES), F32),
         ]
-        + [pltpu.VMEM((pieces * edges, LANES), F32)] * TABLES,
+        + [pltpu.VMEM((sides * owners * edges, LANES), F32)] * TABLES,
         compiler_params=pltpu.CompilerParams(vmem_limit_bytes=58 << 20),
         cost_estimate=pl.CostEstimate(flops=20 * 10**9, transcendentals=0, bytes_accessed=10**7),
         name=name,
@@ -315,45 +386,62 @@
     )
 
 
-def slot_blocks(basis_vals, keep_mask):
-    count, slots, edges = basis_vals.shape
-    weighted = basis_vals * keep_mask.astype(BF16)[None]
-    split = weighted.reshape(count, slots, edges // BLOCK, BLOCK)
-    return jnp.transpose(split, (2, 0, 1, 3)).reshape(edges // BLOCK, count, slots * BLOCK)
-
-
-def edge_reduce(rows):
+def edge_fields():
     count = lax.axis_size("edge")
-    rank = lax.axis_index("edge")
-    steps = []
+    fields = []
     size = 1
     while size < count:
-        steps.append(size)
-        size *= 2
-    total = rows.shape[0]
-    padded = -(-total // (16 * count)) * 16 * count
-    value = jnp.pad(rows, ((0, padded - total), (0, 0)))
-    for mask in steps:
-        half = value.shape[0] // 2
-        bit = (rank & mask) != 0
-        keep = jnp.where(bit, value[half:], value[:half])
-        send = jnp.where(bit, value[:half], value[half:])
-        got = edge_swap(send, mask)
-        value = (keep.astype(F32) + got.astype(F32)).astype(BF16)
-    for mask in reversed(steps):
-        bit = (rank & mask) != 0
-        got = edge_swap(value, mask)
-        value = jnp.concatenate(
-            [jnp.where(bit, got, value), jnp.where(bit, value, got)], axis=0
-        )
-    return value[:total]
-
-
-def edge_sum(value, kind):
+        width = min(8, count // size)
+        fields.append((size, width))
+        size *= width
+    return fields
+
+
+def edge_scatter(value):
+    rank = lax.axis_index("edge")
+    for size, width in edge_fields():
+        place = (rank // size) % width
+        chunks = value.reshape(width, -1, value.shape[1])
+        total = pick(chunks, place).astype(F32)
+        for mask in range(1, width):
+            total = total + edge_swap(pick(chunks, place ^ mask), mask * size).astype(F32)
+        value = total.astype(BF16)
+    return value
+
+
+def edge_gather(value):
+    rank = lax.axis_index("edge")
+    for size, width in reversed(edge_fields()):
+        mask = 1
+        while mask < width:
+            bit = (rank & (mask * size)) != 0
+            got = edge_swap(value, mask * size)
+            value = jnp.concatenate(
+                [jnp.where(bit, got, value), jnp.where(bit, value, got)], axis=0
+            )
+            mask *= 2
+    return value
+
+
+def tree_sum(values):
+    values = [value.astype(F32) for value in values]
+    while len(values) > 1:
+        values = [values[i] + values[i + 1] for i in range(0, len(values), 2)]
+    return values[0]
+
+
+def edge_total(value):
+    for size, width in edge_fields():
+        got = [value] + [edge_swap(value, mask * size) for mask in range(1, width)]
+        value = tree_sum(got).astype(BF16)
+    return value
+
+
+def edge_sum(value):
     count = lax.axis_size("edge")
     size = 1
     while size < count:
-        value = value + edge_swap(value.astype(kind), size).astype(F32)
+        value = value + edge_swap(value, size)
         size *= 2
     return value
 
@@ -405,7 +493,8 @@
     def own(array, axis):
         return lax.dynamic_slice_in_dim(array, start, edges, axis)
 
-    own_edges = jnp.concatenate(exchange(edge_emb.reshape(parts, edges, cols), rank), axis=1)
+    edge_blocks = edge_emb.reshape(parts, edges, cols)
+    own_edges = jnp.concatenate(exchange(edge_blocks, rank), axis=1)
 
     trip_cols = triplet_down_weight.shape[1]
     quad_cols = quad_down.shape[1]
@@ -467,34 +556,69 @@
     trip_rows = trip_piece.shape[0]
     wire = jnp.concatenate([trip_piece, quad_piece], axis=0)
     before = edge_shift(wire, 1)
-    after_wire = edge_shift(wire, -1)
-    own_pieces = gather_chan(wire)
-    sides = jnp.stack([before, after_wire])
-    across = chan_swap(sides, 2)
-    beside = chan_swap(jnp.stack([sides, across]), 1)
-    side_pieces = [sides, beside[0], across, beside[1]]
-    all_pieces = jnp.stack(
-        [side[0] for side in side_pieces] + own_pieces + [side[1] for side in side_pieces]
-    )
-    trip_packed = all_pieces[:, :trip_rows]
-    quad_packed = all_pieces[:, trip_rows:]
-
-    large = jnp.concatenate(
-        [
-            trip_up,
-            quad_up,
-            source_proj,
-            target_proj,
-            resid_first,
-            columns(resid_second),
-            columns(edge_to_atom),
-        ],
-        axis=0,
-    )
-    large_rel = gather_chan(after(large, across))
-    large = reorder(large_rel, rank)
-    grad_blocks = after(grad_edges, large_rel[2]).reshape(parts, edges, cols)
-    grad_two = jnp.concatenate(exchange(grad_blocks, rank), axis=1)
+    later = edge_shift(wire, -1)
+    own_across = chan_swap(wire, 2)
+    own_beside = chan_swap(wire, 1)
+
+    def spread(first, across):
+        return [first, chan_swap(first, 1), across, chan_swap(across, 1)]
+
+    before_across = chan_swap(before, 2)
+    later_across = chan_swap(later, 2)
+    wire_pieces = (
+        spread(before, before_across)
+        + [wire, own_beside, own_across, chan_swap(own_across, 1)]
+        + spread(later, later_across)
+    )
+
+    def places(source):
+        local = own(source, 1)
+        within = local % edges_here
+        owner = (within // edges) ^ rank
+        return ((local // edges_here) * edges_here + owner * edges + within % edges).reshape(-1)
+
+    trip_index = places(trip_source)
+    quad_index = places(quad_source)
+    trip_basis, quad_basis = slot_basis(
+        after(rank, wire), circular, trip_mask, spherical, quad_mask, edges
+    )
+
+    members = gate(
+        [trip_up, quad_up, source_proj, target_proj, resid_first, resid_second, edge_to_atom], wire
+    )
+    large = jnp.concatenate(members[:5] + [columns(members[5]), columns(members[6])], axis=0)
+    tag_onehot = (atom_tags[:, None] == jnp.arange(TAGS)[None, :]).astype(F32)
+    atom_full = after(atom_emb, wire).astype(F32) + jnp.dot(
+        tag_onehot, tag_table.astype(F32), precision=HIGHEST
+    )
+    atom_low = atom_full.astype(BF16)
+    grad_blocks = after(grad_edges, wire).reshape(parts, edges, cols)
+    grad_sent = [pick(grad_blocks, rank ^ step) for step in range(parts)]
+    quad_agg, quad_sum = branch_forward(
+        after(quad_index, large, atom_low, *grad_sent),
+        wire_pieces,
+        trip_rows,
+        quad_basis,
+        quad_bil,
+        "quad_gather",
+    )
+    large_across, large_beside, atom_before, atom_later = gate(
+        [chan_swap(large, 2), chan_swap(large, 1), edge_shift(atom_low, 1), edge_shift(atom_low, -1)],
+        quad_agg,
+    )
+
+    trip_agg, trip_sum = branch_forward(
+        after(trip_index, large_across, atom_before, atom_later),
+        wire_pieces,
+        0,
+        trip_basis,
+        trip_bil,
+        "trip_gather",
+    )
+    grad_got = [grad_sent[0]] + [chan_swap(grad_sent[step], step) for step in range(1, parts)]
+    large_diag, *grad_got = gate([chan_swap(large_across, 1)] + grad_got, trip_agg)
+    large = reorder([large, large_beside, large_across, large_diag], rank)
+    grad_two = jnp.concatenate(reorder(grad_got, rank), axis=1)
     sizes = [
         trip_up.shape[0],
         quad_up.shape[0],
@@ -526,14 +650,7 @@
         [uncolumns(block, edge_to_atom.shape[1]) for block in piece(6)], axis=0
     )
 
-    tag_onehot = (atom_tags[:, None] == jnp.arange(TAGS)[None, :]).astype(F32)
-    atom_full = atom_emb.astype(F32) + jnp.dot(
-        tag_onehot, tag_table.astype(F32), precision=HIGHEST
-    )
-    atom_low = atom_full.astype(BF16)
-    atom_wide = jnp.concatenate(
-        [edge_shift(atom_low, 1), atom_low, edge_shift(atom_low, -1)], axis=0
-    )
+    atom_wide = jnp.concatenate([atom_before, atom_low, atom_later], axis=0)
     atom_total = edge_parts * atoms_here
     source_local = (own(edge_source, 0) - (edge_rank - 1) * atoms_here) % atom_total
     target_local = own(edge_target, 0) - edge_rank * atoms_here
@@ -545,24 +662,6 @@
             matmul(target_hot, atom_low).astype(BF16),
         ],
         axis=1,
-    )
-
-    def places(source):
-        local = own(source, 1)
-        within = local % edges_here
-        owner = (within // edges) ^ rank
-        return ((local // edges_here) * edges_here + owner * edges + within % edges).reshape(-1)
-
-    trip_index = places(trip_source)
-    quad_index = places(quad_source)
-    circular, spherical = lax.optimization_barrier((circular, spherical, wire))[:2]
-    trip_basis = slot_blocks(own(circular, 2), own(trip_mask, 1))
-    quad_basis = slot_blocks(own(spherical, 2), own(quad_mask, 1))
-    trip_agg, trip_sum = branch_forward(
-        trip_index, trip_packed, trip_basis, trip_bil, "trip_gather"
-    )
-    quad_agg, quad_sum = branch_forward(
-        quad_index, quad_packed, quad_basis, quad_bil, "quad_gather"
     )
 
     message = matmul(ends, proj_full)
@@ -630,17 +729,25 @@
     def split(array, axis):
         return jnp.split(array, parts, axis=axis)
 
-    def share(members):
+    def pack(members):
         packed = [
             jnp.concatenate([member[i] for member in members], axis=0).astype(BF16)
             for i in range(parts)
         ]
-        packed = reorder(packed, rank)
-        got = chan_swap(jnp.stack([packed[1], packed[3]]), 1).astype(F32)
-        mine = packed[0].astype(F32) + got[0]
-        return mine, (packed[2].astype(F32) + got[1]).astype(BF16)
-
-    mine, other = share(
+        return reorder(packed, rank)
+
+    def ungroup(array, folds):
+        groups, rows, out = array.shape
+        array = array.reshape(groups, folds, rows // folds, out)
+        return jnp.transpose(array, (1, 0, 2, 3)).reshape(groups * folds, rows // folds, out)
+
+    trip_bilinear_grad = ungroup(
+        jnp.einsum("gej,eo->gjo", trip_sum, trip_agg_grad, preferred_element_type=F32), trip_folds
+    )
+    quad_bilinear_grad = ungroup(
+        jnp.einsum("gej,eo->gjo", quad_sum, quad_agg_grad, preferred_element_type=F32), quad_folds
+    )
+    packed = pack(
         [
             split(trip_up_grad, 1),
             split(quad_up_grad, 1),
@@ -649,63 +756,85 @@
             split(resid_first_grad, 1),
             [columns(block) for block in split(resid_second_grad, 0)],
             [columns(block) for block in split(edge_to_atom_grad, 0)],
+            [fold_lanes(block.reshape(-1, trip_out)) for block in split(trip_bilinear_grad, 1)],
+            [fold_lanes(block.reshape(-1, quad_out)) for block in split(quad_bilinear_grad, 1)],
         ]
     )
-    other_got = chan_swap(other, 2)
     atom_rows = jnp.concatenate(
         [columns(atom_update_grad), columns(output_first_grad)], axis=0
     ).astype(BF16)
-
+    atom_quarter = pick(atom_rows.reshape(parts, -1, LANES), rank)
+
+    def send_back(array):
+        blocks = jnp.stack([array[:, i * cols : (i + 1) * cols] for i in range(parts)])
+        return [pick(blocks, rank ^ step) for step in range(parts)]
+
+    def receive(sent):
+        return [sent[0]] + [chan_swap(sent[step], step) for step in range(1, parts)]
+
+    out_sent = send_back(edges_low)
+    one_sent = send_back(one_grad.astype(BF16))
     wide_low = wide_atoms.astype(BF16)
-    wide_atoms = wide_atoms + chan_swap(wide_low, 1).astype(F32)
-    wide_low = wide_atoms.astype(BF16)
-    wide_atoms = wide_atoms + chan_swap(wide_low, 2).astype(F32)
-    atom_grad = (
-        atoms_new_grad
-        + wide_atoms[1]
-        + edge_shift(wide_atoms[0].astype(BF16), -1).astype(F32)
-        + edge_shift(wide_atoms[2].astype(BF16), 1).astype(F32)
-    )
-    tag_table_grad = jnp.dot(tag_onehot.T, atom_grad, precision=HIGHEST)
-
-    pieces = 3 * parts
-
-    def fold_table(table):
-        table = table.reshape(3, parts, -1, LANES)
-        got = chan_swap(jnp.stack([table[:, 1], table[:, 3]]), 1).astype(F32)
-        mine = table[:, 0].astype(F32) + got[0]
-        return mine, (table[:, 2].astype(F32) + got[1]).astype(BF16)
-
-    def return_table(mine):
-        to_before = edge_shift(mine[0].astype(BF16), -1)
-        to_after = edge_shift(mine[2].astype(BF16), 1)
-        return mine[1] + to_before.astype(F32) + to_after.astype(F32)
-
-    trip_table = branch_backward(
-        after(trip_index, other), trip_basis, trip_agg_grad, trip_bil, pieces, "trip_scatter"
-    )
-    trip_mine, trip_other = fold_table(trip_table)
-    trip_got = chan_swap(trip_other, 2)
-    quad_table = branch_backward(
-        after(quad_index, trip_other), quad_basis, quad_agg_grad, quad_bil, pieces, "quad_scatter"
-    )
-    trip_grad = return_table(trip_mine + trip_got.astype(F32))
-    quad_mine, quad_other = fold_table(quad_table)
-    quad_grad = return_table(quad_mine + chan_swap(quad_other, 2).astype(F32))
+
+    trip_tables = branch_backward(
+        after(trip_index, wide_low, *packed, *out_sent, *one_sent),
+        trip_basis,
+        trip_agg_grad,
+        trip_bil,
+        3,
+        parts,
+        "trip_scatter",
+    )
+    arrived = gate(
+        [chan_swap(packed[1], 1), chan_swap(packed[3], 1), chan_swap(wide_low, 1)]
+        + receive(out_sent)
+        + receive(one_sent),
+        trip_tables[0],
+    )
+    mine = packed[0].astype(F32) + arrived[0].astype(F32)
+    other = (packed[2].astype(F32) + arrived[1].astype(F32)).astype(BF16)
+    wide_low = (wide_low.astype(F32) + arrived[2].astype(F32)).astype(BF16)
+    edges_out = jnp.concatenate(reorder(arrived[3 : 3 + parts], rank), axis=0)
+    one_out = jnp.concatenate(reorder(arrived[3 + parts :], rank), axis=0)
+
+    quad_tables = branch_backward(
+        after(quad_index, wide_low, other, edges_out, one_out, *trip_tables),
+        quad_basis,
+        quad_agg_grad,
+        quad_bil,
+        3,
+        parts,
+        "quad_scatter",
+    )
+    other_got, wide_got, *trip_got = gate(
+        [chan_swap(other, 2), chan_swap(wide_low, 2)] + receive(trip_tables), quad_tables[0]
+    )
+    quad_got = receive(quad_tables)
+    mine = (mine + other_got.astype(F32)).astype(BF16)
+    early = mine.shape[0]
+    early_rows = jnp.concatenate([mine, atom_quarter], axis=0)
+    total_rows = early_rows.shape[0]
+    unit = 16 * edge_parts
+    early_rows = jnp.pad(early_rows, ((0, -total_rows % unit), (0, 0)))
+    early_part = edge_scatter(early_rows)
+
+    table = jnp.concatenate([tree_sum(trip_got), tree_sum(quad_got)], axis=1)
+    branch_grad = (
+        table[1]
+        + edge_shift(table[0].astype(BF16), -1).astype(F32)
+        + edge_shift(table[2].astype(BF16), 1).astype(F32)
+    )
     branch_grad = jnp.concatenate(
-        [unfold_lanes(trip_grad, trip_width), unfold_lanes(quad_grad, quad_width)], axis=1
+        [
+            unfold_lanes(branch_grad[:trip_rows], trip_width),
+            unfold_lanes(branch_grad[trip_rows:], quad_width),
+        ],
+        axis=1,
     )
     down_grad = (branch_grad * radial_pre * silu_grad(down_pre)).astype(BF16)
     radial_grad = (branch_grad * jax.nn.silu(down_pre)).astype(BF16)
     down_weight_grad = inner(own_edges, down_grad)
     radial_weight_grad = inner(own_radial, radial_grad)
-
-    def give_back(array):
-        blocks = jnp.stack([array[:, i * cols : (i + 1) * cols] for i in range(parts)])
-        return jnp.concatenate(exchange(blocks, rank), axis=0)
-
-    edges_out = give_back(edges_low)
-    one_out = give_back(one_grad.astype(BF16)).astype(F32)
     down_wire = jnp.concatenate(
         [fold_lanes(down_grad[:, :trip_width]), fold_lanes(down_grad[:, trip_width:])], axis=0
     )
@@ -724,44 +853,39 @@
         axis=0,
     )
     down_rows = lax.dynamic_slice_in_dim(down_full, rank * cols, cols, 0)
-    edge_grad = one_out + outer(down_all, down_rows)
-
-    mine = (mine + other_got.astype(F32)).astype(BF16)
-    early = mine.shape[0]
-    summed = edge_reduce(jnp.concatenate([mine, atom_rows], axis=0)).astype(F32)
-
-    def ungroup(array, folds):
-        groups, rows, out = array.shape
-        array = array.reshape(groups, folds, rows // folds, out)
-        return jnp.transpose(array, (1, 0, 2, 3)).reshape(groups * folds, rows // folds, out)
-
-    trip_bilinear_grad = ungroup(
-        jnp.einsum("gej,eo->gjo", trip_sum, trip_agg_grad, preferred_element_type=F32), trip_folds
-    )
-    quad_bilinear_grad = ungroup(
-        jnp.einsum("gej,eo->gjo", quad_sum, quad_agg_grad, preferred_element_type=F32), quad_folds
-    )
+    down_all, down_rows = gate([down_all, down_rows])
+    edge_grad = one_out.astype(F32) + outer(down_all, down_rows)
+
+    wide_sum = wide_low.astype(F32) + wide_got.astype(F32)
+    atom_grad = (
+        atoms_new_grad
+        + wide_sum[1]
+        + edge_shift(wide_sum[0].astype(BF16), -1).astype(F32)
+        + edge_shift(wide_sum[2].astype(BF16), 1).astype(F32)
+    )
+    tag_table_grad = jnp.dot(tag_onehot.T, atom_grad, precision=HIGHEST)
+    tiny = edge_sum(jnp.concatenate([output_second_grad[None], tag_table_grad], axis=0))
+
     small_grad = jnp.concatenate([down_weight_grad, radial_weight_grad], axis=0)
-    late_mine, late_other = share(
+    late_sent = pack(
         [
             [
                 columns(jnp.concatenate([trip_block, quad_block], axis=1).T)
                 for trip_block, quad_block in zip(
                     split(small_grad[:, :trip_width], 1), split(small_grad[:, trip_width:], 1)
                 )
-            ],
-            [fold_lanes(block.reshape(-1, trip_out)) for block in split(trip_bilinear_grad, 1)],
-            [fold_lanes(block.reshape(-1, quad_out)) for block in split(quad_bilinear_grad, 1)],
+            ]
         ]
     )
-    late = late_mine + chan_swap(late_other, 2).astype(F32)
-    late = edge_sum(late, BF16)
-    tiny = edge_sum(jnp.concatenate([output_second_grad[None], tag_table_grad], axis=0), F32)
+    late = edge_total(tree_sum(receive(late_sent)).astype(BF16)).astype(F32)
+    summed = edge_gather(early_part)[:total_rows]
+    atom_out = jnp.concatenate(reorder(gather_direct(summed[early:]), rank), axis=0).astype(F32)
+    summed = summed[:early].astype(F32)
+    sizes = sizes + [trip_bil_rows, quad_bilinear.size // LANES]
+    offsets = offsets_of(sizes)
     parts_out = [summed[offsets[i] : offsets[i + 1]] for i in range(len(sizes))]
-    small_out = uncolumns(late[:small_rows], long).T
-    trip_bil_out = late[small_rows : small_rows + trip_bil_rows]
-    quad_bil_out = late[small_rows + trip_bil_rows :]
-    atom_out = summed[early:]
+    small_out = uncolumns(late, long).T
+    trip_bil_out, quad_bil_out = parts_out[7:]
     half = atom_out.shape[0] // 2
     return (
         edges_out,

time: 466 us -> 439 us (0.942)
  local copies, waits for them, and re-layouts: 77.7 us -> 30.3 us
  matrix products: 91.1 us -> 52.1 us
  starting transfers between devices: 43.9 us -> 72.8 us
  other arithmetic: 40.5 us -> 55.6 us
  waiting for transfers between devices: 98.5 us -> 106 us
  Pallas kernels: 104 us -> 110 us
    dot_general x9, matrix products: 58.2 us -> 18.3 us  [outer(): lax.dot_general(first_op, second_op, (((1,), (1,)), ((), ())), preferred_...]
    concatenate x7 -> x10, other arithmetic: 2.21 us -> 35.7 us  [the longest x1 34.2 us: per_device(): jnp.concatenate([jnp.concatenate([unfold_lanes(block[:trip_rows], trip_wi...]
    ppermute x12 -> x20, starting transfers between devices: 5.82 us -> 27.1 us  [edge_swap(): return lax.ppermute(value, 'edge', [(i, i ^ mask) for i in range(count)])]
    unnamed x479 -> x417, local copies, waits for them, and re-layouts: 31.2 us -> 10.3 us
    ppermute x35 -> x48, waiting for transfers between devices: 56.9 us -> 72.8 us  [chan_swap(): return lax.ppermute(value, 'chan', [(i, i ^ mask) for i in range(count)])]
    ppermute x10 -> x8, waiting for transfers between devices: 27.7 us -> 12.8 us  [edge_shift(): lax.ppermute(value, 'edge', [(i, (i + step) % count) for i in range(count)])]
    reshape x7 -> x0, local copies, waits for them, and re-layouts: 13.7 us -> none  [the longest x1 5.55 us: slot_blocks(): split = weighted.reshape(count, slots, edges // BLOCK, BLOCK)]
    ppermute x35 -> x48, starting transfers between devices: 21.9 us -> 30.1 us  [chan_swap(): return lax.ppermute(value, 'chan', [(i, i ^ mask) for i in range(count)])]
  transfers between devices with their start and end apart: 57 -> 76, of which waited for: 24 -> 24; matrix products, arithmetic and copies ran while one was open for 25% -> 16% of each run, Pallas kernels for 23% -> 26%
where the time goes in v1:
time: 439 us; the launch traced here: 431 us
  Pallas kernels  110 us (25%)
  waiting for transfers between devices  106 us (24%)
  starting transfers between devices  72.8 us (17%)
  other arithmetic  55.6 us (13%)
  matrix products  52.1 us (12%)
  local copies, waits for them, and re-layouts  30.3 us (7%)
    ppermute x48, waiting for transfers between devices, chan_swap(): return lax.ppermute(value, 'chan', [(i, i ^ mask) for i in range(count)])  72.8 us
    pallas_call x2, Pallas kernels, branch_backward(): pl.pallas_call(functools.partial(scatter_body, folds=folds, owners=owners...  57.4 us
    pallas_call x2, Pallas kernels, branch_forward(): pl.pallas_call(functools.partial(gather_body, folds=folds, first_row=firs...  46.7 us
    concatenate x1, other arithmetic, per_device(): jnp.concatenate([jnp.concatenate([unfold_lanes(block[:trip_rows], trip_wi...  34.2 us
    ppermute x48, starting transfers between devices, chan_swap(): return lax.ppermute(value, 'chan', [(i, i ^ mask) for i in range(count)])  30.1 us
    ppermute x20, starting transfers between devices, edge_swap(): return lax.ppermute(value, 'edge', [(i, i ^ mask) for i in range(count)])  27.1 us
    ppermute x20, waiting for transfers between devices, edge_swap(): return lax.ppermute(value, 'edge', [(i, i ^ mask) for i in range(count)])  20.1 us
    dot_general x9, matrix products, outer(): lax.dot_general(first_op, second_op, (((1,), (1,)), ((), ())), preferred_...  18.3 us
  transfers between devices with their start and end apart: 76, of which 24 were waited for; matrix products, arithmetic and copies ran while one was open for 16% of the time, Pallas kernels for 26%

profile of v1, /device:TPU:0, one launch (start us, length us, event | category | flops | bytes accessed | tf_op | source)
XLA Modules:
  0.0 431.3 jit_solution(5621482502845837974)
XLA Ops:
  18.1 5.3 %collective-permute-done = bf16[1024,128]{1,0:T(8,128)(2,1)S(1)} collective-permute-done((bf16[1024,128]{1,0:T(8,128)(2,1)S(1)}, bf16[1024,128]{1,0:T(8,128)(2,1)S(1)}, u32[]{:S(2)}, u32[]{:S(2)}) %collective-permute-start) | collective-permute-done | bytes 262176 | tf_op jit(solution)/shard_map/ppermute | solution.py:20
  27.1 4.5 %collective-permute-start.17 = (bf16[768,128]{1,0:T(8,128)(2,1)}, bf16[768,128]{1,0:T(8,128)(2,1)}, u32[]{:S(2)}, u32[]{:S(2)}) collective-permute-start(bf16[768,128]{1,0:T(8,128)(2,1)} %maximum_maximum_fusion.4.refs_4_), channel_id=1, source_target_pairs={{0,28},{4,0},{8,4},{12,8},{16,12},{20,16},{24,20},{28,24},{1,29},{... | collective-permute-start | bytes 589832 | tf_op jit(solution)/shard_map/ppermute | solution.py:30
  34.1 6.3 %slot_basis.1 = (bf16[64,16,256]{2,1,0:T(8,128)(2,1)}, bf16[64,32,128]{2,1,0:T(8,128)(2,1)}) custom-call(s32[1]{0:T(128)} %bitcast.25.rank_ref, bf16[16,16,4096]{2,1,0:T(8,128)(2,1)} %trip_vals.1, s32[16,4096]{1,0:T(8,128)} %trip_keep.1, bf16[32,8,4096]{2,1,0:T(8,128)(2,1)} %quad_vals.1, s32[8,4096]{1,0:T(8,128)} %quad_keep.1), custom_call_target="tpu_custom_call" | custom-call | flops 10000000000 | bytes 10000000 | tf_op jit(solution)/shard_map/slot_basis/pallas_call | solution.py:245
  44.6 3.9 collective-permute-done.19.refs_10_
  48.5 3.7 collective-permute-done.12.refs_2_
  52.7 4.5 %collective-permute-start.9 = (bf16[128,256]{1,0:T(8,128)(2,1)S(1)}, bf16[128,256]{1,0:T(8,128)(2,1)S(1)}, u32[]{:S(2)}, u32[]{:S(2)}) collective-permute-start(bf16[128,256]{1,0:T(8,128)(2,1)S(1)} %get-tuple-element.452), channel_id=1, source_target_pairs={{0,28},{4,0},{8,4},{12,8},{16,12},{20,16},{24,20},{28,24},{1,29},{... | collective-permute-start | bytes 196616 | tf_op jit(solution)/shard_map/ppermute | solution.py:30
  59.7 19.1 %quad_gather.1 = (bf16[1024,32]{1,0:T(8,128)(2,1)}, bf16[8,1024,128]{2,1,0:T(8,128)(2,1)}) custom-call(s32[8192]{0:T(1024)} %bitcast.351, bf16[64,32,128]{2,1,0:T(8,128)(2,1)} %get-tuple-element.101.basis_ref, bf16[8,128,32]{2,1,0:T(8,128)(2,1)} %bitcast.314, bf16[768,128]{1,0:T(8,128)(2,1)} %collective-permute-done.10.refs_0_, ...), custom_call_target="tpu_custom_call" | custom-call | flops 20000000000 | bytes 10000000 | tf_op jit(solution)/shard_map/quad_gather/pallas_call | solution.py:181
  80.4 27.6 %trip_gather.1 = (bf16[1024,64]{1,0:T(8,128)(2,1)}, bf16[8,1024,128]{2,1,0:T(8,128)(2,1)}) custom-call(s32[16384]{0:T(1024)} %bitcast.349, bf16[64,16,256]{2,1,0:T(8,128)(2,1)} %get-tuple-element.107.basis_ref, bf16[8,128,64]{2,1,0:T(8,128)(2,1)} %bitcast.316, bf16[768,128]{1,0:T(8,128)(2,1)} %collective-permute-done.10.refs_0_, ...), custom_call_target="tpu_custom_call" | custom-call | flops 20000000000 | bytes 10000000 | tf_op jit(solution)/shard_map/trip_gather/pallas_call | solution.py:181
  114.4 4.7 %multiply_add_fusion = (f32[1024,512]{1,0:T(8,128)S(1)}, f32[1024,512]{1,0:T(8,128)}) fusion(f32[1024,512]{1,0:T(8,128)S(1)} %fusion.130, f32[1024,512]{1,0:T(8,128)S(1)} %fusion.127, bf16[1024,128]{1,0:T(8,128)(2,1)S(1)} %get-tuple-element.183, bf16[1024,128]{1,0:T(8,128)(2,1)S(1)} %get-tuple-element.182, bf16[1024,128]{1,0:T(8,128)(2,1)S(1)} %get-tuple-element.181, ...), kind=kOutput, calls=%fused_computation.10 | convolution fusion | flops 555220992 | bytes 11010048 | tf_op jit(solution)/shard_map/dot_general | solution.py:75
  133.2 13.1 %collective-permute-done.26 = f32[128,256]{1,0:T(8,128)S(1)} collective-permute-done((f32[128,256]{1,0:T(8,128)S(1)}, f32[128,256]{1,0:T(8,128)S(1)}, u32[]{:S(2)}, u32[]{:S(2)}) %collective-permute-start.26) | collective-permute-done | bytes 131104 | tf_op jit(solution)/shard_map/ppermute | solution.py:20
  159.1 3.6 fusion.151
  187.9 32.8 %trip_scatter.1 = (bf16[3,512,128]{2,1,0:T(8,128)(2,1)}, bf16[3,512,128]{2,1,0:T(8,128)(2,1)}, bf16[3,512,128]{2,1,0:T(8,128)(2,1)}, bf16[3,512,128]{2,1,0:T(8,128)(2,1)}) custom-call(s32[16384]{0:T(1024)} %bitcast.350, bf16[64,16,256]{2,1,0:T(8,128)(2,1)} %get-tuple-element.107.basis_ref, bf16[1024,64]{1,0:T(8,128)(2,1)} %copy-done.35, ...), custom_call_target="tpu_custom_call" | custom-call | flops 20000000000 | bytes 10000000 | tf_op jit(solution)/shard_map/trip_scatter/pallas_call | solution.py:347
  224.0 5.7 %collective-permute-done.35 = bf16[1024,128]{1,0:T(8,128)(2,1)S(1)} collective-permute-done((bf16[1024,128]{1,0:T(8,128)(2,1)S(1)}, bf16[1024,128]{1,0:T(8,128)(2,1)S(1)}, u32[]{:S(2)}, u32[]{:S(2)}) %collective-permute-start.35) | collective-permute-done | bytes 262176 | tf_op jit(solution)/shard_map/ppermute | solution.py:20
  230.8 5.1 %collective-permute-done.34 = bf16[1024,128]{1,0:T(8,128)(2,1)S(1)} collective-permute-done((bf16[1024,128]{1,0:T(8,128)(2,1)S(1)}, bf16[1024,128]{1,0:T(8,128)(2,1)S(1)}, u32[]{:S(2)}, u32[]{:S(2)}) %collective-permute-start.34) | collective-permute-done | bytes 262176 | tf_op jit(solution)/shard_map/ppermute | solution.py:20
  240.8 24.6 %quad_scatter.1 = (bf16[3,256,128]{2,1,0:T(8,128)(2,1)}, bf16[3,256,128]{2,1,0:T(8,128)(2,1)}, bf16[3,256,128]{2,1,0:T(8,128)(2,1)}, bf16[3,256,128]{2,1,0:T(8,128)(2,1)}) custom-call(s32[8192]{0:T(1024)} %bitcast.352, bf16[64,32,128]{2,1,0:T(8,128)(2,1)} %get-tuple-element.101.basis_ref, bf16[1024,32]{1,0:T(8,128)(2,1)} %copy-done.10, ...), custom_call_target="tpu_custom_call" | custom-call | flops 20000000000 | bytes 10000000 | tf_op jit(solution)/shard_map/quad_scatter/pallas_call | solution.py:347
  268.9 4.5 %collective-permute-done.42 = bf16[3,256,128]{2,1,0:T(8,128)(2,1)S(1)} collective-permute-done((bf16[3,256,128]{2,1,0:T(8,128)(2,1)}, bf16[3,256,128]{2,1,0:T(8,128)(2,1)S(1)}, u32[]{:S(2)}, u32[]{:S(2)}) %collective-permute-start.42) | collective-permute-done | bytes 196640 | tf_op jit(solution)/shard_map/ppermute | solution.py:20
  273.6 22.9 %collective-permute-done.43 = bf16[3,256,128]{2,1,0:T(8,128)(2,1)S(1)} collective-permute-done((bf16[3,256,128]{2,1,0:T(8,128)(2,1)}, bf16[3,256,128]{2,1,0:T(8,128)(2,1)S(1)}, u32[]{:S(2)}, u32[]{:S(2)}) %collective-permute-start.43) | collective-permute-done | bytes 196640 | tf_op jit(solution)/shard_map/ppermute | solution.py:20
  297.8 5.8 %collective-permute-done.37 = bf16[3,128,256]{2,1,0:T(8,128)(2,1)S(1)} collective-permute-done((bf16[3,128,256]{2,1,0:T(8,128)(2,1)S(1)}, bf16[3,128,256]{2,1,0:T(8,128)(2,1)S(1)}, u32[]{:S(2)}, u32[]{:S(2)}) %collective-permute-start.37) | collective-permute-done | bytes 196640 | tf_op jit(solution)/shard_map/ppermute | solution.py:20
  303.7 4.5 %collective-permute-start.48 = (bf16[128,256]{1,0:T(8,128)(2,1)S(1)}, bf16[128,256]{1,0:T(8,128)(2,1)S(1)}, u32[]{:S(2)}, u32[]{:S(2)}) collective-permute-start(bf16[128,256]{1,0:T(8,128)(2,1)S(1)} %get-tuple-element.370), channel_id=1, source_target_pairs={{0,28},{4,0},{8,4},{12,8},{16,12},{20,16},{24,20},{28,24},{1,29},{... | collective-permute-start | bytes 196616 | tf_op jit(solution)/shard_map/ppermute | solution.py:30
  310.2 5.2 %collective-permute-done.49 = bf16[128,256]{1,0:T(8,128)(2,1)S(1)} collective-permute-done((bf16[128,256]{1,0:T(8,128)(2,1)S(1)}, bf16[128,256]{1,0:T(8,128)(2,1)S(1)}, u32[]{:S(2)}, u32[]{:S(2)}) %collective-permute-start.49) | collective-permute-done | bytes 65568 | tf_op jit(solution)/shard_map/ppermute | solution.py:30
  324.9 4.3 %collective-permute-start.63 = (bf16[304,128]{1,0:T(8,128)(2,1)S(1)}, bf16[304,128]{1,0:T(8,128)(2,1)S(1)}, u32[]{:S(2)}, u32[]{:S(2)}) collective-permute-start(bf16[304,128]{1,0:T(8,128)(2,1)S(1)} %get-tuple-element.243), channel_id=1, source_target_pairs={{0,16},{4,20},{8,24},{12,28},{16,0},{20,4},{24,8},{28,12},{1,17},{... | collective-permute-start | bytes 233480 | tf_op jit(solution)/shard_map/ppermute | solution.py:25
  356.6 5.2 %collective-permute-start.56 = (bf16[120,128]{1,0:T(8,128)(2,1)S(1)}, bf16[120,128]{1,0:T(8,128)(2,1)S(1)}, u32[]{:S(2)}, u32[]{:S(2)}) collective-permute-start(bf16[120,128]{1,0:T(8,128)(2,1)S(1)} %add_convert_fusion.7), channel_id=1, source_target_pairs={{0,16},{4,20},{8,24},{12,28},{16,0},{20,4},{24,8},{28,12},{1,17},{... | collective-permute-start | bytes 92168 | tf_op jit(solution)/shard_map/ppermute | solution.py:25
  373.5 11.1 %collective-permute-done.69 = bf16[1216,128]{1,0:T(8,128)(2,1)S(1)} collective-permute-done((bf16[1216,128]{1,0:T(8,128)(2,1)S(1)}, bf16[1216,128]{1,0:T(8,128)(2,1)S(1)}, u32[]{:S(2)}, u32[]{:S(2)}) %collective-permute-start.69) | collective-permute-done | bytes 311328 | tf_op jit(solution)/shard_map/ppermute | solution.py:25
  394.9 34.2 %maximum_maximum_fusion = bf16[4096,96]{1,0:T(8,128)(2,1)S(1)} fusion(bf16[256,32]{1,0:T(8,128)(2,1)S(1)} %get-tuple-element.393, bf16[256,32]{1,0:T(8,128)(2,1)S(1)} %get-tuple-element.394, bf16[256,32]{1,0:T(8,128)(2,1)S(1)} %get-tuple-element.395, bf16[256,32]{1,0:T(8,128)(2,1)S(1)} %get-tuple-element.392, bf16[512,64]{1,0:T(8,128)(2,1)S(1)} %get-tuple-element.391, ...), kind=kLoop, calls=%fused_computation.60 | loop fusion | flops 18874368 | bytes 1572864 | tf_op jit(solution)/shard_map/concatenate | solution.py:842
  (761 shorter events, 164.7 us)
Async XLA Ops:
  27.1 13.3 %collective-permute-start.17 = (bf16[768,128]{1,0:T(8,128)(2,1)}, bf16[768,128]{1,0:T(8,128)(2,1)}, u32[]{:S(2)}, u32[]{:S(2)}) collective-permute-start(bf16[768,128]{1,0:T(8,128)(2,1)} %maximum_maximum_fusion.4.refs_4_), channel_id=1, source_target_pairs={{0,28},{4,0},{8,4},{12,8},{16,12},{20,16},{24,20},{28,24},{1,29},{... | collective-permute-start | bytes 589832 | tf_op jit(solution)/shard_map/ppermute | solution.py:30
  52.7 26.1 %collective-permute-start.9 = (bf16[128,256]{1,0:T(8,128)(2,1)S(1)}, bf16[128,256]{1,0:T(8,128)(2,1)S(1)}, u32[]{:S(2)}, u32[]{:S(2)}) collective-permute-start(bf16[128,256]{1,0:T(8,128)(2,1)S(1)} %get-tuple-element.452), channel_id=1, source_target_pairs={{0,28},{4,0},{8,4},{12,8},{16,12},{20,16},{24,20},{28,24},{1,29},{... | collective-permute-start | bytes 196616 | tf_op jit(solution)/shard_map/ppermute | solution.py:30
  57.2 22.7 %collective-permute-start.8 = (bf16[128,256]{1,0:T(8,128)(2,1)S(1)}, bf16[128,256]{1,0:T(8,128)(2,1)S(1)}, u32[]{:S(2)}, u32[]{:S(2)}) collective-permute-start(bf16[128,256]{1,0:T(8,128)(2,1)S(1)} %get-tuple-element.452), channel_id=1, source_target_pairs={{0,4},{4,8},{8,12},{12,16},{16,20},{20,24},{24,28},{28,0},{1,5},{5... | collective-permute-start | bytes 196616 | tf_op jit(solution)/shard_map/ppermute | solution.py:30
  57.2 22.9 %collective-permute-start.7 = (bf16[1888,128]{1,0:T(8,128)(2,1)S(1)}, bf16[1888,128]{1,0:T(8,128)(2,1)S(1)}, u32[]{:S(2)}, u32[]{:S(2)}) collective-permute-start(bf16[1888,128]{1,0:T(8,128)(2,1)S(1)} %constant_dynamic-update-slice_fusion.27), channel_id=1, source_target_pairs={{0,1},{1,0},{2,3},{3,2},{4,5},{5,4},{6,7},{7,6},{8,9},{9,8},{10,11... | collective-permute-start | bytes 1449992 | tf_op jit(solution)/shard_map/ppermute | solution.py:20
  57.5 22.6 %collective-permute-start.6 = (bf16[1888,128]{1,0:T(8,128)(2,1)S(1)}, bf16[1888,128]{1,0:T(8,128)(2,1)S(1)}, u32[]{:S(2)}, u32[]{:S(2)}) collective-permute-start(bf16[1888,128]{1,0:T(8,128)(2,1)S(1)} %constant_dynamic-update-slice_fusion.27), channel_id=1, source_target_pairs={{0,2},{1,3},{2,0},{3,1},{4,6},{5,7},{6,4},{7,5},{8,10},{9,11},{10,... | collective-permute-start | bytes 1449992 | tf_op jit(solution)/shard_map/ppermute | solution.py:20
  59.0 50.5 %collective-permute-start.24 = (bf16[1024,128]{1,0:T(8,128)(2,1)}, bf16[1024,128]{1,0:T(8,128)(2,1)S(1)}, u32[]{:S(2)}, u32[]{:S(2)}) collective-permute-start(bf16[1024,128]{1,0:T(8,128)(2,1)} %get-tuple-element.216), channel_id=1, source_target_pairs={{0,3},{1,2},{2,1},{3,0},{4,7},{5,6},{6,5},{7,4},{8,11},{9,10},{10,... | collective-permute-start | bytes 786440 | tf_op jit(solution)/shard_map/ppermute | solution.py:20
  78.8 30.7 %collective-permute-start.23 = (bf16[1024,128]{1,0:T(8,128)(2,1)S(1)}, bf16[1024,128]{1,0:T(8,128)(2,1)S(1)}, u32[]{:S(2)}, u32[]{:S(2)}) collective-permute-start(bf16[1024,128]{1,0:T(8,128)(2,1)S(1)} %get-tuple-element.217), channel_id=1, source_target_pairs={{0,2},{1,3},{2,0},{3,1},{4,6},{5,7},{6,4},{7,5},{8,10},{9,11},{10,... | collective-permute-start | bytes 786440 | tf_op jit(solution)/shard_map/ppermute | solution.py:20
  79.9 29.6 %collective-permute-start.22 = (bf16[1024,128]{1,0:T(8,128)(2,1)S(1)}, bf16[1024,128]{1,0:T(8,128)(2,1)S(1)}, u32[]{:S(2)}, u32[]{:S(2)}) collective-permute-start(bf16[1024,128]{1,0:T(8,128)(2,1)S(1)} %get-tuple-element.218), channel_id=1, source_target_pairs={{0,1},{1,0},{2,3},{3,2},{4,5},{5,4},{6,7},{7,6},{8,9},{9,8},{10,11... | collective-permute-start | bytes 786440 | tf_op jit(solution)/shard_map/ppermute | solution.py:20
  80.1 29.4 %collective-permute-start.21 = (bf16[1888,128]{1,0:T(8,128)(2,1)S(1)}, bf16[1888,128]{1,0:T(8,128)(2,1)S(1)}, u32[]{:S(2)}, u32[]{:S(2)}) collective-permute-start(bf16[1888,128]{1,0:T(8,128)(2,1)S(1)} %collective-permute-done.6), channel_id=1, source_target_pairs={{0,1},{1,0},{2,3},{3,2},{4,5},{5,4},{6,7},{7,6},{8,9},{9,8},{10,11... | collective-permute-start | bytes 1449992 | tf_op jit(solution)/shard_map/ppermute | solution.py:20
  129.1 92.4 %collective-permute-start.32 = (bf16[1024,128]{1,0:T(8,128)(2,1)}, bf16[1024,128]{1,0:T(8,128)(2,1)}, u32[]{:S(2)}, u32[]{:S(2)}) collective-permute-start(bf16[1024,128]{1,0:T(8,128)(2,1)} %get-tuple-element.204), channel_id=1, source_target_pairs={{0,3},{1,2},{2,1},{3,0},{4,7},{5,6},{6,5},{7,4},{8,11},{9,10},{10,... | collective-permute-start | bytes 786440 | tf_op jit(solution)/shard_map/ppermute | solution.py:20
  130.0 91.6 %collective-permute-start.31 = (bf16[1024,128]{1,0:T(8,128)(2,1)}, bf16[1024,128]{1,0:T(8,128)(2,1)}, u32[]{:S(2)}, u32[]{:S(2)}) collective-permute-start(bf16[1024,128]{1,0:T(8,128)(2,1)} %get-tuple-element.205), channel_id=1, source_target_pairs={{0,2},{1,3},{2,0},{3,1},{4,6},{5,7},{6,4},{7,5},{8,10},{9,11},{10,... | collective-permute-start | bytes 786440 | tf_op jit(solution)/shard_map/ppermute | solution.py:20
  131.0 91.6 %collective-permute-start.30 = (bf16[1024,128]{1,0:T(8,128)(2,1)}, bf16[1024,128]{1,0:T(8,128)(2,1)}, u32[]{:S(2)}, u32[]{:S(2)}) collective-permute-start(bf16[1024,128]{1,0:T(8,128)(2,1)} %get-tuple-element.206), channel_id=1, source_target_pairs={{0,1},{1,0},{2,3},{3,2},{4,5},{5,4},{6,7},{7,6},{8,9},{9,8},{10,11... | collective-permute-start | bytes 786440 | tf_op jit(solution)/shard_map/ppermute | solution.py:20
  131.0 15.3 %collective-permute-start.26 = (f32[128,256]{1,0:T(8,128)S(1)}, f32[128,256]{1,0:T(8,128)S(1)}, u32[]{:S(2)}, u32[]{:S(2)}) collective-permute-start(f32[128,256]{1,0:T(8,128)S(1)} %add.355), channel_id=1, source_target_pairs={{0,2},{1,3},{2,0},{3,1},{4,6},{5,7},{6,4},{7,5},{8,10},{9,11},{10,... | collective-permute-start | bytes 393224 | tf_op jit(solution)/shard_map/ppermute | solution.py:20
  184.3 39.5 %collective-permute-start.29 = (bf16[3,128,256]{2,1,0:T(8,128)(2,1)}, bf16[3,128,256]{2,1,0:T(8,128)(2,1)}, u32[]{:S(2)}, u32[]{:S(2)}) collective-permute-start(bf16[3,128,256]{2,1,0:T(8,128)(2,1)} %convert_element_type.327), channel_id=1, source_target_pairs={{0,1},{1,0},{2,3},{3,2},{4,5},{5,4},{6,7},{7,6},{8,9},{9,8},{10,11... | collective-permute-start | bytes 589832 | tf_op jit(solution)/shard_map/ppermute | solution.py:20
  220.9 15.8 %collective-permute-start.28 = (bf16[2080,128]{1,0:T(8,128)(2,1)S(1)}, bf16[2080,128]{1,0:T(8,128)(2,1)S(1)}, u32[]{:S(2)}, u32[]{:S(2)}) collective-permute-start(bf16[2080,128]{1,0:T(8,128)(2,1)S(1)} %get-tuple-element.169), channel_id=1, source_target_pairs={{0,1},{1,0},{2,3},{3,2},{4,5},{5,4},{6,7},{7,6},{8,9},{9,8},{10,11... | collective-permute-start | bytes 1597448 | tf_op jit(solution)/shard_map/ppermute | solution.py:20
  221.5 15.3 %collective-permute-start.27 = (bf16[2080,128]{1,0:T(8,128)(2,1)S(1)}, bf16[2080,128]{1,0:T(8,128)(2,1)S(1)}, u32[]{:S(2)}, u32[]{:S(2)}) collective-permute-start(bf16[2080,128]{1,0:T(8,128)(2,1)S(1)} %get-tuple-element.171), channel_id=1, source_target_pairs={{0,1},{1,0},{2,3},{3,2},{4,5},{5,4},{6,7},{7,6},{8,9},{9,8},{10,11... | collective-permute-start | bytes 1597448 | tf_op jit(solution)/shard_map/ppermute | solution.py:20
  229.6 68.2 %collective-permute-start.38 = (bf16[3,512,128]{2,1,0:T(8,128)(2,1)}, bf16[3,512,128]{2,1,0:T(8,128)(2,1)S(1)}, u32[]{:S(2)}, u32[]{:S(2)}) collective-permute-start(bf16[3,512,128]{2,1,0:T(8,128)(2,1)} %get-tuple-element.129), channel_id=1, source_target_pairs={{0,1},{1,0},{2,3},{3,2},{4,5},{5,4},{6,7},{7,6},{8,9},{9,8},{10,11... | collective-permute-start | bytes 1179656 | tf_op jit(solution)/shard_map/ppermute | solution.py:20
  235.9 61.9 %collective-permute-start.39 = (bf16[3,512,128]{2,1,0:T(8,128)(2,1)}, bf16[3,512,128]{2,1,0:T(8,128)(2,1)}, u32[]{:S(2)}, u32[]{:S(2)}) collective-permute-start(bf16[3,512,128]{2,1,0:T(8,128)(2,1)} %get-tuple-element.130), channel_id=1, source_target_pairs={{0,2},{1,3},{2,0},{3,1},{4,6},{5,7},{6,4},{7,5},{8,10},{9,11},{10,... | collective-permute-start | bytes 1179656 | tf_op jit(solution)/shard_map/ppermute | solution.py:20
  267.4 36.3 %collective-permute-start.36 = (bf16[2080,128]{1,0:T(8,128)(2,1)S(1)}, bf16[2080,128]{1,0:T(8,128)(2,1)S(1)}, u32[]{:S(2)}, u32[]{:S(2)}) collective-permute-start(bf16[2080,128]{1,0:T(8,128)(2,1)S(1)} %add_convert_fusion.2), channel_id=1, source_target_pairs={{0,2},{1,3},{2,0},{3,1},{4,6},{5,7},{6,4},{7,5},{8,10},{9,11},{10,... | collective-permute-start | bytes 1597448 | tf_op jit(solution)/shard_map/ppermute | solution.py:20
  268.2 29.6 %collective-permute-start.40 = (bf16[3,512,128]{2,1,0:T(8,128)(2,1)}, bf16[3,512,128]{2,1,0:T(8,128)(2,1)S(1)}, u32[]{:S(2)}, u32[]{:S(2)}) collective-permute-start(bf16[3,512,128]{2,1,0:T(8,128)(2,1)} %get-tuple-element.131), channel_id=1, source_target_pairs={{0,3},{1,2},{2,1},{3,0},{4,7},{5,6},{6,5},{7,4},{8,11},{9,10},{10,... | collective-permute-start | bytes 1179656 | tf_op jit(solution)/shard_map/ppermute | solution.py:20
  273.5 23.0 %collective-permute-start.43 = (bf16[3,256,128]{2,1,0:T(8,128)(2,1)}, bf16[3,256,128]{2,1,0:T(8,128)(2,1)S(1)}, u32[]{:S(2)}, u32[]{:S(2)}) collective-permute-start(bf16[3,256,128]{2,1,0:T(8,128)(2,1)} %get-tuple-element.140), channel_id=1, source_target_pairs={{0,3},{1,2},{2,1},{3,0},{4,7},{5,6},{6,5},{7,4},{8,11},{9,10},{10,... | collective-permute-start | bytes 589832 | tf_op jit(solution)/shard_map/ppermute | solution.py:20
  315.8 13.4 %collective-permute-start.60 = (bf16[304,128]{1,0:T(8,128)(2,1)S(1)}, bf16[304,128]{1,0:T(8,128)(2,1)S(1)}, u32[]{:S(2)}, u32[]{:S(2)}) collective-permute-start(bf16[304,128]{1,0:T(8,128)(2,1)S(1)} %get-tuple-element.239), channel_id=1, source_target_pairs={{0,4},{4,0},{8,12},{12,8},{16,20},{20,16},{24,28},{28,24},{1,5},{5... | collective-permute-start | bytes 233480 | tf_op jit(solution)/shard_map/ppermute | solution.py:25
  370.8 13.7 %collective-permute-start.69 = (bf16[1216,128]{1,0:T(8,128)(2,1)S(1)}, bf16[1216,128]{1,0:T(8,128)(2,1)S(1)}, u32[]{:S(2)}, u32[]{:S(2)}) collective-permute-start(bf16[1216,128]{1,0:T(8,128)(2,1)S(1)} %pad_maximum_fusion.12), channel_id=1, source_target_pairs={{0,16},{4,20},{8,24},{12,28},{16,0},{20,4},{24,8},{28,12},{1,17},{... | collective-permute-start | bytes 933896 | tf_op jit(solution)/shard_map/ppermute | solution.py:25
  373.4 20.5 %collective-permute-start.47 = (bf16[2,768,128]{2,1,0:T(8,128)(2,1)S(1)}, bf16[2,768,128]{2,1,0:T(8,128)(2,1)S(1)}, u32[]{:S(2)}, u32[]{:S(2)}) collective-permute-start(bf16[2,768,128]{2,1,0:T(8,128)(2,1)S(1)} %pad_maximum_fusion.11), channel_id=1, source_target_pairs={{0,1},{1,0},{2,3},{3,2},{4,5},{5,4},{6,7},{7,6},{8,9},{9,8},{10,11... | collective-permute-start | bytes 1179656 | tf_op jit(solution)/shard_map/ppermute | solution.py:20
  (228 other events, 2216.4 us)
